TPU v7x, 512 devices: a whole 4x4x16 slice. The times are simulated.
512 devices in a mesh: sector: 16 (over y, x), grp: 32 (over z, core).
Axes of the slice: x: 4, y: 4, z: 16, core: 2. Of those that a mesh axis runs over, the one named last changes fastest.
Arguments:
- start_vector: bfloat16 [8192, 512], P(('sector', 'grp')), may hold values from -130 to 130
- tile_live: int32 [64], P('sector'), may hold values from 32 to 128, as said below
- env_blocks: bfloat16 [64, 384, 128, 128], P('grp', 'sector'), may hold values from -2 to 4
- block_owner: int32 [64, 384, 1], P('grp', 'sector'), may hold values from 0 to 15; in each aligned block of 24 rows (0 to 23, 24 to 47, ..., all dimensions but the last counted through in order) at most 2 rows name the same one
- block_rows: int32 [64, 384], P('grp', 'sector'), may hold values from 0 to 3
- block_cols: int32 [64, 384], P('grp', 'sector'), may hold values from 0 to 3
- site_left: bfloat16 [64, 1024], P('grp'), may hold values from -0.375 to 0.375
- mpo_pattern: int32 [64, 64], P('grp'), may hold values 0 or 1
- site_right: bfloat16 [64, 1024], P('grp'), may hold values from -0.375 to 0.375
- right_env: bfloat16 [64, 1024], P('grp'), may hold values from -0.125 to 0.125
Outputs:
- first_product: bfloat16 [8192, 512], P(('sector', 'grp'))
- second_product: bfloat16 [8192, 512], P(('sector', 'grp'))
Inputs may be any that keep to these rules, and one draw needn't show every extreme that they name: `tile_live`: rows beyond a tile's live count are padding; some tile is full. `block_owner`: in each aligned block of 24 entries of one channel (the blocks one device holds), no owner is named more than 2 times.
All inputs are finite; a program needn't handle non-finite values. No bound on the sum of `mpo_pattern` on one device may be relied on, other than what follows from the above.
Results may differ from a plain program's by a relative error of at most 0.03.
Values may be sent and summed in bfloat16 or wider, within the bound.
A program may use at most 64 MiB of HBM per device.

v0:
```python
import jax
import jax.numpy as jnp
from jax import lax
from jax.sharding import PartitionSpec as P

WM = 64
D1 = 4
RB = 32
TR = 128
TPO = 4
CAP = 2
PHYS = 16


epsilon = 1e-06


def contract(owned_rows, got_blocks, got_codes):
    channels = got_blocks.shape[0]
    slot_count = got_blocks.shape[1] * got_blocks.shape[2]
    results = []
    for channel in range(channels):
        blocks = got_blocks[channel].reshape(slot_count, TR * TR)
        slot_codes = got_codes[channel].reshape(slot_count)
        tile_index = jnp.maximum(slot_codes - 1, 0)
        pair_hot = (
            (tile_index[:, None] == jnp.arange(TPO * TPO, dtype=jnp.int32)[None, :])
            & (slot_codes[:, None] > 0)
        ).astype(jnp.bfloat16)
        summed = jnp.einsum(
            "sp,sq->pq", pair_hot, blocks, preferred_element_type=jnp.float32
        ).astype(jnp.bfloat16)
        dense = summed.reshape(TPO, TPO, TR, TR).transpose(0, 2, 1, 3).reshape(TPO * TR, TPO * TR)
        product = jnp.dot(dense, owned_rows, preferred_element_type=jnp.float32)
        results.append(product.astype(jnp.bfloat16))
    return jnp.stack(results)


def owner_gather(share_rows):
    return lax.all_gather(share_rows, "grp", axis=0, tiled=True)


def channel_share(mixed_rows, mixing):
    return lax.psum_scatter(
        jnp.einsum("wrk,wkn->rn", mixed_rows, mixing, preferred_element_type=jnp.float32).astype(
            jnp.bfloat16
        ),
        "grp",
        scatter_dimension=0,
        tiled=True,
    ).astype(jnp.float32)


def local(
    start_vector,
    tile_live,
    env_blocks,
    block_owner,
    block_rows,
    block_cols,
    site_left,
    mpo_pattern,
    site_right,
    right_env,
):
    sectors = lax.axis_size("sector")
    groups = lax.axis_size("grp")
    share_count = start_vector.shape[0]
    columns = start_vector.shape[1]
    channels = env_blocks.shape[0]
    held_blocks = env_blocks.shape[1]
    right_site, right_panels = (
        lax.all_gather(site_right, "grp", axis=0, tiled=True),
        lax.all_gather(right_env, "grp", axis=0, tiled=True),
    )
    left_site = (
        site_left.reshape(channels, WM, D1, D1) * mpo_pattern.astype(jnp.bfloat16)[:, :, None, None]
    )
    joined = jnp.einsum(
        "wmac,mxbd->wxabcd",
        left_site,
        right_site.reshape(WM, WM, D1, D1),
        preferred_element_type=jnp.float32,
    ).astype(jnp.bfloat16)
    mixing = jnp.einsum(
        "wxq,xr->wqr",
        joined.reshape(channels, WM, PHYS * PHYS),
        right_panels,
        preferred_element_type=jnp.float32,
    ).astype(jnp.bfloat16)
    mixing = (
        mixing.reshape(channels, PHYS, PHYS, RB, RB)
        .transpose(0, 2, 3, 1, 4)
        .reshape(channels, columns, columns)
    )
    owners = block_owner[:, :, 0]
    owner_hot = (owners[:, :, None] == jnp.arange(sectors, dtype=jnp.int32)[None, None, :]).astype(
        jnp.int32
    )
    position = jnp.sum((jnp.cumsum(owner_hot, axis=1) - owner_hot) * owner_hot, axis=2)
    slot_index = owners * CAP + position
    select = slot_index[:, :, None] == jnp.arange(sectors * CAP, dtype=jnp.int32)[None, None, :]
    packed = jnp.einsum(
        "wes,wen->wsn",
        select.astype(jnp.bfloat16),
        env_blocks.reshape(channels, held_blocks, TR * TR),
        preferred_element_type=jnp.float32,
    ).astype(jnp.bfloat16)
    slot_codes = jnp.sum(
        select.astype(jnp.int32) * (1 + block_rows * TPO + block_cols)[:, :, None], axis=1
    )
    got_blocks, got_codes = (
        lax.all_to_all(
            packed.reshape(channels, sectors, CAP, TR * TR),
            "sector",
            split_axis=1,
            concat_axis=1,
            tiled=True,
        ),
        lax.all_to_all(
            slot_codes.reshape(channels, sectors, CAP),
            "sector",
            split_axis=1,
            concat_axis=1,
            tiled=True,
        ),
    )
    tile_mask = (jnp.arange(TR, dtype=jnp.int32)[None, :] < tile_live[:, None]).reshape(TPO * TR)
    owner_mask = tile_mask.astype(jnp.float32)[:, None]
    share_mask = lax.dynamic_slice_in_dim(
        owner_mask, lax.axis_index("grp") * share_count, share_count, 0
    )
    entry_count = float(sectors * groups * share_count * columns)
    owned_rows = owner_gather(start_vector) * owner_mask.astype(jnp.bfloat16)
    first_mixed = contract(owned_rows, got_blocks, got_codes)
    owner_total = lax.psum(
        jnp.einsum("wrk,wkn->rn", first_mixed, mixing, preferred_element_type=jnp.float32).astype(
            jnp.bfloat16
        ),
        "grp",
    ).astype(jnp.float32)
    owner_first = (owner_total * owner_mask).astype(jnp.bfloat16)
    first_product = lax.dynamic_slice_in_dim(
        owner_first, lax.axis_index("grp") * share_count, share_count, 0
    )
    widened = first_product.astype(jnp.float32)
    squares = lax.psum(jnp.sum(widened * widened), ("sector", "grp"))
    inverse_norm = lax.rsqrt(squares / entry_count + epsilon)
    second_mixed = contract(owner_first, got_blocks, got_codes)
    second_product = (channel_share(second_mixed, mixing) * inverse_norm * share_mask).astype(jnp.bfloat16)
    return (first_product, second_product)


def solution(mesh):
    in_specs = (
        P(("sector", "grp"), None),
        P("sector"),
        P("grp", "sector", None, None),
        P("grp", "sector", None),
        P("grp", "sector"),
        P("grp", "sector"),
        P("grp", None),
        P("grp", None),
        P("grp", None),
        P("grp", None),
    )
    out_specs = (P(("sector", "grp"), None), P(("sector", "grp"), None))
    return jax.shard_map(local, mesh=mesh, in_specs=in_specs, out_specs=out_specs, check_vma=False)
```

profile of v0, /device:TPU:4, one launch (start us, length us, event | category | flops | bytes accessed | tf_op | source)
XLA Modules:
  0.0 513.1 jit_solution(16789400535820442056)
XLA Ops:
  11.0 9.1 %all-to-all-start = ((s32[2,16,2]{2,0,1:T(2,128)}), s32[2,16,2]{2,0,1:T(2,128)S(1)}, u32[]{:S(2)}, u32[]{:S(2)}) async-start(s32[2,16,2]{2,0,1:T(2,128)} %copy.24), calls=%async_computation | async-start | bytes 32768 | tf_op jit(solution)/shard_map/all_to_all | solution.py:120
  20.2 3.7 reshape.113
  23.9 2.2 convolution_convert_fusion
  26.1 2.7 reshape.114
  28.8 5.5 %copy.25 = bf16[2,16,2,16384]{3,2,0,1:T(2,128)(2,1)} copy(bf16[2,16,2,16384]{3,2,1,0:T(2,128)(2,1)} %reshape.114) | data formatting | bytes 4194304 | tf_op jit(solution)/shard_map/reshape | solution.py:114
  34.2 7.4 %all-to-all-start.1 = ((bf16[2,16,2,16384]{3,2,0,1:T(2,128)(2,1)}), bf16[2,16,2,16384]{3,2,0,1:T(2,128)(2,1)S(1)}, u32[]{:S(2)}, u32[]{:S(2)}) async-start(bf16[2,16,2,16384]{3,2,0,1:T(2,128)(2,1)} %copy.25), calls=%async_computation.1 | async-start | bytes 4194304 | tf_op jit(solution)/shard_map/all_to_all | solution.py:113
  41.7 34.9 %all-gather = bf16[32,2,1024]{2,1,0:T(2,128)(2,1)S(1)} all-gather(bf16[1,2,1024]{2,1,0:T(2,128)(2,1)S(1)} %bitcast.91), channel_id=1, replica_groups=mesh['sector'=16,'grp'=32] {'grp'}, dimensions={0}, use_global_device_ids=true | all-gather | bytes 135168 | tf_op jit(solution)/shard_map/all_gather | solution.py:73
  76.6 10.0 %reshape.119 = bf16[64,64,4,4]{3,2,1,0:T(4,128)(2,1)} reshape(bf16[32,2,1024]{2,1,0:T(2,128)(2,1)S(1)} %all-gather) | data formatting | bytes 262144 | tf_op jit(solution)/shard_map/reshape | solution.py:82
  86.6 6.4 %copy.34 = bf16[64,64,4,4,1,1]{1,0,3,2,5,4:T(8,128)(2,1)S(1)} copy(bf16[64,64,4,4,1,1]{3,2,1,0,5,4:T(4,128)(2,1)} %bitcast.79) | data formatting | bytes 262144 | tf_op jit(solution)/shard_map/reshape | solution.py:82
  94.1 27.6 %all-gather.1 = bf16[32,2,1024]{2,1,0:T(2,128)(2,1)S(1)} all-gather(bf16[1,2,1024]{2,1,0:T(2,128)(2,1)S(1)} %bitcast.92), channel_id=1, replica_groups=mesh['sector'=16,'grp'=32] {'grp'}, dimensions={0}, use_global_device_ids=true | all-gather | bytes 135168 | tf_op jit(solution)/shard_map/all_gather | solution.py:74
  122.2 4.3 reshape.121
  126.6 9.0 %copy.32 = bf16[2,16,32,16,32]{4,3,2,1,0:T(8,128)(2,1)} copy(bf16[2,16,32,16,32]{4,2,1,3,0:T(8,128)(2,1)} %bitcast.78) | data formatting | bytes 2097152 | tf_op jit(solution)/shard_map/transpose | solution.py:93
  135.5 6.8 %reshape.122 = bf16[2,512,512]{2,1,0:T(8,128)(2,1)} reshape(bf16[2,16,32,16,32]{4,3,2,1,0:T(8,128)(2,1)} %copy.32) | data formatting | bytes 2097152 | tf_op jit(solution)/shard_map/reshape | solution.py:94
  142.4 32.7 %all_gather.9 = bf16[512,512]{1,0:T(8,128)(2,1)} all-gather(bf16[16,512]{1,0:T(8,128)(2,1)S(1)} %copy-done.2), channel_id=1, replica_groups=mesh['sector'=16,'grp'=32] {'grp'}, dimensions={0}, use_global_device_ids=true | all-gather | bytes 540672 | tf_op jit(solution)/shard_map/all_gather | solution.py:40
  175.6 2.4 fusion.42
  178.0 1.5 reshape_squeeze.5
  183.1 1.5 fusion
  184.7 206.9 %all-reduce.2.cloned.1.call-done = bf16[512,512]{1,0:T(8,128)(2,1)} async-done(((bf16[512,512]{1,0:T(8,128)(2,1)}), bf16[512,512]{1,0:T(8,128)(2,1)}) %all-reduce.2.cloned.1.call-update) | async-done | bytes 524304 | tf_op jit(solution)/shard_map/psum | solution.py:136
  391.6 1.2 multiply_convert_fusion
  393.7 1.5 fusion.1
  395.3 1.2 multiply_reduce_fusion
  396.5 104.5 %psum.15 = f32[]{:T(128)} all-reduce(f32[]{:T(128)} %get-tuple-element.6), channel_id=1, replica_groups=mesh['sector'=16,'grp'=32] {'sector','grp'}, use_global_device_ids=true, to_apply=%region_6.7 | all-reduce | flops 1 | bytes 8 | tf_op jit(solution)/shard_map/psum | solution.py:147
  501.7 3.2 reduce-scatter.2.cloned.1.call-done
  504.9 1.4 multiply_convert_fusion.1
  (58 shorter events, 10.5 us)
Async XLA Ops:
  11.0 23.2 %all-to-all-start = ((s32[2,16,2]{2,0,1:T(2,128)}), s32[2,16,2]{2,0,1:T(2,128)S(1)}, u32[]{:S(2)}, u32[]{:S(2)}) async-start(s32[2,16,2]{2,0,1:T(2,128)} %copy.24), calls=%async_computation | async-start | bytes 32768 | tf_op jit(solution)/shard_map/all_to_all | solution.py:120
  34.2 7.5 %copy-start.3 = (bf16[2,1024]{1,0:T(2,128)(2,1)S(1)}, bf16[2,1024]{1,0:T(2,128)(2,1)}, u32[]{:S(2)}) copy-start(bf16[2,1024]{1,0:T(2,128)(2,1)} %param.18) | copy-start | bytes 12292
  34.2 141.4 %all-to-all-start.1 = ((bf16[2,16,2,16384]{3,2,0,1:T(2,128)(2,1)}), bf16[2,16,2,16384]{3,2,0,1:T(2,128)(2,1)S(1)}, u32[]{:S(2)}, u32[]{:S(2)}) async-start(bf16[2,16,2,16384]{3,2,0,1:T(2,128)(2,1)} %copy.25), calls=%async_computation.1 | async-start | bytes 4194304 | tf_op jit(solution)/shard_map/all_to_all | solution.py:113
  41.7 349.9 %all-reduce.2.cloned.1.call-start = ((), (), s32[]{:S(2)}) async-start(), calls=%async_computation.3 | async-start | bytes 1048576 | tf_op jit(solution)/shard_map/psum | solution.py:136
  86.5 6.5 %copy-start.7 = (s32[2,64]{1,0:T(2,128)S(1)}, s32[2,64]{1,0:T(2,128)}, u32[]{:S(2)}) copy-start(s32[2,64]{1,0:T(2,128)} %param.17) | copy-start | bytes 1540
  86.6 6.9 %copy-start.4 = (bf16[2,1024]{1,0:T(2,128)(2,1)S(1)}, bf16[2,1024]{1,0:T(2,128)(2,1)}, u32[]{:S(2)}) copy-start(bf16[2,1024]{1,0:T(2,128)(2,1)} %param.16) | copy-start | bytes 12292
  86.6 7.5 %copy-start.5 = (bf16[2,1024]{1,0:T(2,128)(2,1)S(1)}, bf16[2,1024]{1,0:T(2,128)(2,1)}, u32[]{:S(2)}) copy-start(bf16[2,1024]{1,0:T(2,128)(2,1)} %param.19) | copy-start | bytes 12292
  135.5 6.8 %copy-start.6 = (s32[4]{0:T(128)S(1)}, s32[4]{0:T(128)}, u32[]{:S(2)}) copy-start(s32[4]{0:T(128)} %param.11) | copy-start | bytes 52
  135.5 6.9 %copy-start.2 = (bf16[16,512]{1,0:T(8,128)(2,1)S(1)}, bf16[16,512]{1,0:T(8,128)(2,1)}, u32[]{:S(2)}) copy-start(bf16[16,512]{1,0:T(8,128)(2,1)} %param.10) | copy-start | bytes 49156
  180.9 1.0 copy-start.1
  181.8 1.2 copy-start
  184.6 320.2 %reduce-scatter.2.cloned.1.call-start = ((), (), s32[]{:S(2)}) async-start(), calls=%async_computation.4 | async-start | bytes 540672 | tf_op jit(solution)/shard_map/reduce_scatter | solution.py:44
Sparse Core Ops, SparseCore 0:
  184.8 206.7 all-reduce.1
  395.3 109.4 reduce-scatter.1
where the time goes:
time: 514 us; the launch traced here: 513 us
  waiting for transfers between devices  210 us (41%)
  blocking collectives  200 us (39%)
  local copies, waits for them, and re-layouts  55.9 us (11%)
  starting transfers between devices  16.6 us (3%)
  between operations  15 us (3%)
  matrix products  8.67 us (2%)
  other arithmetic  7.16 us (1%)
    psum x1, waiting for transfers between devices, local(): lax.psum(jnp.einsum('wrk,wkn->rn', first_mixed, mixing, preferred_element...  207 us
    psum x1, blocking collectives, local(): squares = lax.psum(jnp.sum(widened * widened), ('sector', 'grp'))  105 us
    all_gather x1, blocking collectives, local(): lax.all_gather(site_right, 'grp', axis=0, tiled=True)  34.9 us
    all_gather x1, blocking collectives, owner_gather(): return lax.all_gather(share_rows, 'grp', axis=0, tiled=True)  32.7 us
    all_gather x1, blocking collectives, local(): lax.all_gather(right_env, 'grp', axis=0, tiled=True)  27.6 us
    reshape x2, local copies, waits for them, and re-layouts, local(): right_site.reshape(WM, WM, D1, D1)  16.4 us
  transfers between devices with their start and end apart: 4, of which 2 were waited for; matrix products, arithmetic and copies ran while one was open for 11% of the time, Pallas kernels for 0%

commit v1 on v0

--- a/solution.py
+++ b/solution.py
@@ -1,6 +1,10 @@
+import functools
+
 import jax
 import jax.numpy as jnp
 from jax import lax
+from jax.experimental import pallas as pl
+from jax.experimental.pallas import tpu as pltpu
 from jax.sharding import PartitionSpec as P
 
 WM = 64
@@ -15,7 +19,354 @@
 epsilon = 1e-06
 
 
-def contract(owned_rows, got_blocks, got_codes):
+MESH = pl.DeviceIdType.MESH
+SHARE = 16
+
+
+def send_to(src, dst, send_sem, recv_sem, target):
+    return pltpu.make_async_remote_copy(
+        src_ref=src,
+        dst_ref=dst,
+        send_sem=send_sem,
+        recv_sem=recv_sem,
+        device_id=target,
+        device_id_type=MESH,
+    )
+
+
+def greet(chips, chip, core, sectors=0):
+    barrier = pltpu.get_barrier_semaphore()
+
+    def greet_chip(step, carry):
+        other = lax.rem(chip + step, chips)
+        pl.semaphore_signal(
+            barrier, inc=1, device_id={"grp": other * 2 + core}, device_id_type=MESH
+        )
+        return carry
+
+    lax.fori_loop(1, chips, greet_chip, 0)
+    pl.semaphore_signal(
+        barrier, inc=1, device_id={"grp": chip * 2 + 1 - core}, device_id_type=MESH
+    )
+    if sectors:
+        owner = lax.axis_index("sector")
+
+        def greet_owner(step, carry):
+            pl.semaphore_signal(
+                barrier,
+                inc=1,
+                device_id={"sector": lax.rem(owner + step, sectors)},
+                device_id_type=MESH,
+            )
+            return carry
+
+        lax.fori_loop(1, sectors, greet_owner, 0)
+        pl.semaphore_wait(barrier, chips + sectors - 1)
+    else:
+        pl.semaphore_wait(barrier, chips)
+
+
+def spread(held, chips, chip, core, send_sem, recv_sem, pair_send, pair_recv):
+    sibling = {"grp": chip * 2 + 1 - core}
+    mine = held.at[chip, core]
+
+    def outgoing(step):
+        other = lax.rem(chip + step, chips)
+        return send_to(
+            mine, mine, send_sem.at[step], recv_sem.at[step], {"grp": other * 2 + core}
+        )
+
+    def forward(step):
+        source = lax.rem(chip + chips - step, chips)
+        block = held.at[source, core]
+        return send_to(block, block, pair_send.at[step], pair_recv.at[step], sibling)
+
+    def start(step, carry):
+        outgoing(step).start()
+        return carry
+
+    def relay(step, carry):
+        outgoing(step).wait_recv()
+        forward(step).start()
+        return carry
+
+    def finish(step, carry):
+        outgoing(step).wait_send()
+        return carry
+
+    def finish_pair(step, carry):
+        forward(step).wait()
+        return carry
+
+    lax.fori_loop(1, chips, start, 0)
+    forward(0).start()
+    lax.fori_loop(1, chips, relay, 0)
+    lax.fori_loop(1, chips, finish, 0)
+    lax.fori_loop(0, chips, finish_pair, 0)
+
+
+def gather_kernel(chips, rows_ref, site_ref, env_ref, rows_out, site_out, env_out, *sems):
+    position = lax.axis_index("grp")
+    chip, core = position // 2, lax.rem(position, 2)
+    send_sem, recv_sem, pair_send, pair_recv = sems
+    pairs = ((rows_ref, rows_out), (site_ref, site_out), (env_ref, env_out))
+    for source, target in pairs:
+        target[chip, core] = source[...]
+    greet(chips, chip, core)
+    sibling = {"grp": chip * 2 + 1 - core}
+
+    def outgoing(item, step):
+        other = lax.rem(chip + step, chips)
+        mine = pairs[item][1].at[chip, core]
+        return send_to(
+            mine,
+            mine,
+            send_sem.at[item, step],
+            recv_sem.at[item, step],
+            {"grp": other * 2 + core},
+        )
+
+    def forward(item, step):
+        source = lax.rem(chip + chips - step, chips)
+        block = pairs[item][1].at[source, core]
+        return send_to(block, block, pair_send.at[item, step], pair_recv.at[item, step], sibling)
+
+    def start(step, carry):
+        for item in (1, 2, 0):
+            outgoing(item, step).start()
+        return carry
+
+    def relay(step, carry):
+        for item in (1, 2, 0):
+            outgoing(item, step).wait_recv()
+            forward(item, step).start()
+        return carry
+
+    def finish(step, carry):
+        for item in (1, 2, 0):
+            outgoing(item, step).wait_send()
+        return carry
+
+    def finish_pair(step, carry):
+        for item in (1, 2, 0):
+            forward(item, step).wait()
+        return carry
+
+    lax.fori_loop(1, chips, start, 0)
+    for item in (1, 2, 0):
+        forward(item, 0).start()
+    lax.fori_loop(1, chips, relay, 0)
+    lax.fori_loop(1, chips, finish, 0)
+    lax.fori_loop(0, chips, finish_pair, 0)
+
+
+def gather_all(start_vector, site_right, right_env):
+    chips = lax.axis_size("grp") // 2
+    operands = (start_vector, site_right, right_env)
+    return pl.pallas_call(
+        functools.partial(gather_kernel, chips),
+        out_shape=[jax.ShapeDtypeStruct((chips, 2) + a.shape, a.dtype) for a in operands],
+        in_specs=[pl.BlockSpec(memory_space=pltpu.VMEM)] * 3,
+        out_specs=[pl.BlockSpec(memory_space=pltpu.VMEM)] * 3,
+        scratch_shapes=[pltpu.SemaphoreType.DMA((3, chips))] * 4,
+        compiler_params=pltpu.CompilerParams(collective_id=0, has_side_effects=True),
+    )(*operands)
+
+
+def product(dense_ref, mix_ref, vector, part, base):
+    tile = 256
+
+    def one_tile(index, carry):
+        rows = pl.ds(pl.multiple_of(index * tile, tile), tile)
+        total = jnp.zeros((tile, vector.shape[1]), jnp.float32)
+        for channel in range(dense_ref.shape[0]):
+            mixed = jnp.dot(
+                dense_ref[channel, rows, :], vector, preferred_element_type=jnp.float32
+            ).astype(jnp.bfloat16)
+            total += jnp.dot(mixed, mix_ref[channel], preferred_element_type=jnp.float32)
+        split = total.astype(jnp.bfloat16).reshape(tile // (2 * SHARE), 2, SHARE, vector.shape[1])
+        chunk = pl.ds(index * (tile // (2 * SHARE)), tile // (2 * SHARE))
+        part[base, chunk] = split[:, 0]
+        part[base + 1, chunk] = split[:, 1]
+        return carry
+
+    lax.fori_loop(0, TPO * TR // tile, one_tile, 0)
+
+
+def reduce_share(chips, chip, core, part, base, sib, ready, got, sems):
+    pair_send, pair_recv, send_sem, recv_sem = sems
+    pair = send_to(
+        part.at[base + 1 - core],
+        sib,
+        pair_send,
+        pair_recv,
+        {"grp": chip * 2 + 1 - core},
+    )
+    pair.start()
+    pair.wait()
+    ready[...] = (part[base + core].astype(jnp.float32) + sib[...].astype(jnp.float32)).astype(
+        jnp.bfloat16
+    )
+
+    def outgoing(step):
+        other = lax.rem(chip + step, chips)
+        return send_to(
+            ready.at[other],
+            got.at[step],
+            send_sem.at[step],
+            recv_sem.at[step],
+            {"grp": other * 2 + core},
+        )
+
+    def start(step, carry):
+        outgoing(step).start()
+        return carry
+
+    def collect(step, total):
+        outgoing(step).wait_recv()
+        return total + got[step].astype(jnp.float32)
+
+    def finish(step, carry):
+        outgoing(step).wait_send()
+        return carry
+
+    lax.fori_loop(1, chips, start, 0)
+    total = lax.fori_loop(1, chips, collect, ready[chip].astype(jnp.float32))
+    lax.fori_loop(1, chips, finish, 0)
+    return total
+
+
+def step_kernel(
+    chips,
+    sectors,
+    dense_ref,
+    mix_ref,
+    start_ref,
+    mask_ref,
+    first_out,
+    second_out,
+    part,
+    sib_one,
+    sib_two,
+    ready_one,
+    ready_two,
+    got_one,
+    got_two,
+    held,
+    norm_mine,
+    norm_got,
+    pair_sems,
+    share_sems,
+    spread_sems,
+    norm_sems,
+):
+    position = lax.axis_index("grp")
+    owner = lax.axis_index("sector")
+    chip, core = position // 2, lax.rem(position, 2)
+    rows = TPO * TR
+    columns = start_ref.shape[-1]
+    greet(chips, chip, core, sectors)
+    masked = start_ref[...].reshape(rows, columns) * mask_ref[...].astype(jnp.bfloat16)
+    product(dense_ref, mix_ref, masked, part, 0)
+    share_mask = mask_ref[pl.ds(pl.multiple_of(position * SHARE, SHARE), SHARE), :]
+    total = reduce_share(
+        chips,
+        chip,
+        core,
+        part,
+        0,
+        sib_one,
+        ready_one,
+        got_one,
+        (pair_sems.at[0], pair_sems.at[1], share_sems.at[0], share_sems.at[1]),
+    )
+    first = (total * share_mask).astype(jnp.bfloat16)
+    first_out[...] = first
+    held[chip, core] = first
+    spread(
+        held,
+        chips,
+        chip,
+        core,
+        spread_sems.at[0],
+        spread_sems.at[1],
+        spread_sems.at[2],
+        spread_sems.at[3],
+    )
+    wide = held[...].reshape(rows, columns).astype(jnp.float32)
+    squares = jnp.sum((wide * wide).reshape(rows // 8, 8, columns), axis=0)
+    norm_mine[...] = sum(squares[:, at : at + 128] for at in range(0, columns, 128))
+
+    def norm_copy(step):
+        return send_to(
+            norm_mine,
+            norm_got.at[step],
+            norm_sems.at[0, step],
+            norm_sems.at[1, step],
+            {"sector": lax.rem(owner + step, sectors)},
+        )
+
+    def norm_start(step, carry):
+        norm_copy(step).start()
+        return carry
+
+    def norm_collect(step, carry):
+        norm_copy(step).wait()
+        return carry + norm_got[step]
+
+    lax.fori_loop(1, sectors, norm_start, 0)
+    product(dense_ref, mix_ref, held[...].reshape(rows, columns), part, 2)
+    total = reduce_share(
+        chips,
+        chip,
+        core,
+        part,
+        2,
+        sib_two,
+        ready_two,
+        got_two,
+        (pair_sems.at[2], pair_sems.at[3], share_sems.at[2], share_sems.at[3]),
+    )
+    sums = lax.fori_loop(1, sectors, norm_collect, norm_mine[...])
+    count = float(sectors * rows * columns)
+    inverse_norm = lax.rsqrt(jnp.sum(sums, keepdims=True) / count + epsilon)
+    second_out[...] = (total * inverse_norm * share_mask).astype(jnp.bfloat16)
+
+
+def two_products(dense, mixing, owned_rows, owner_mask):
+    chips = lax.axis_size("grp") // 2
+    sectors = lax.axis_size("sector")
+    columns = owned_rows.shape[-1]
+    shares = pltpu.VMEM((chips, SHARE, columns), jnp.bfloat16)
+    share = jax.ShapeDtypeStruct((SHARE, columns), jnp.bfloat16)
+    return pl.pallas_call(
+        functools.partial(step_kernel, chips, sectors),
+        out_shape=[share, share],
+        in_specs=[pl.BlockSpec(memory_space=pltpu.VMEM)] * 4,
+        out_specs=[pl.BlockSpec(memory_space=pltpu.VMEM)] * 2,
+        scratch_shapes=[
+            pltpu.VMEM((4, chips, SHARE, columns), jnp.bfloat16),
+            shares,
+            shares,
+            shares,
+            shares,
+            shares,
+            shares,
+            pltpu.VMEM((chips, 2, SHARE, columns), jnp.bfloat16),
+            pltpu.VMEM((8, 128), jnp.float32),
+            pltpu.VMEM((sectors, 8, 128), jnp.float32),
+            pltpu.SemaphoreType.DMA((4,)),
+            pltpu.SemaphoreType.DMA((4, chips)),
+            pltpu.SemaphoreType.DMA((4, chips)),
+            pltpu.SemaphoreType.DMA((2, sectors)),
+        ],
+        compiler_params=pltpu.CompilerParams(
+            collective_id=1, has_side_effects=True, vmem_limit_bytes=40 * 1024 * 1024
+        ),
+    )(dense, mixing, owned_rows, owner_mask)
+
+
+def assemble(got_blocks, got_codes):
     channels = got_blocks.shape[0]
     slot_count = got_blocks.shape[1] * got_blocks.shape[2]
     results = []
@@ -30,25 +381,10 @@
         summed = jnp.einsum(
             "sp,sq->pq", pair_hot, blocks, preferred_element_type=jnp.float32
         ).astype(jnp.bfloat16)
-        dense = summed.reshape(TPO, TPO, TR, TR).transpose(0, 2, 1, 3).reshape(TPO * TR, TPO * TR)
-        product = jnp.dot(dense, owned_rows, preferred_element_type=jnp.float32)
-        results.append(product.astype(jnp.bfloat16))
+        results.append(
+            summed.reshape(TPO, TPO, TR, TR).transpose(0, 2, 1, 3).reshape(TPO * TR, TPO * TR)
+        )
     return jnp.stack(results)
-
-
-def owner_gather(share_rows):
-    return lax.all_gather(share_rows, "grp", axis=0, tiled=True)
-
-
-def channel_share(mixed_rows, mixing):
-    return lax.psum_scatter(
-        jnp.einsum("wrk,wkn->rn", mixed_rows, mixing, preferred_element_type=jnp.float32).astype(
-            jnp.bfloat16
-        ),
-        "grp",
-        scatter_dimension=0,
-        tiled=True,
-    ).astype(jnp.float32)
 
 
 def local(
@@ -64,15 +400,11 @@
     right_env,
 ):
     sectors = lax.axis_size("sector")
-    groups = lax.axis_size("grp")
-    share_count = start_vector.shape[0]
     columns = start_vector.shape[1]
     channels = env_blocks.shape[0]
     held_blocks = env_blocks.shape[1]
-    right_site, right_panels = (
-        lax.all_gather(site_right, "grp", axis=0, tiled=True),
-        lax.all_gather(right_env, "grp", axis=0, tiled=True),
-    )
+    owned_rows, right_site, right_panels = gather_all(start_vector, site_right, right_env)
+    right_panels = right_panels.reshape(WM, RB * RB)
     left_site = (
         site_left.reshape(channels, WM, D1, D1) * mpo_pattern.astype(jnp.bfloat16)[:, :, None, None]
     )
@@ -127,28 +459,7 @@
     )
     tile_mask = (jnp.arange(TR, dtype=jnp.int32)[None, :] < tile_live[:, None]).reshape(TPO * TR)
     owner_mask = tile_mask.astype(jnp.float32)[:, None]
-    share_mask = lax.dynamic_slice_in_dim(
-        owner_mask, lax.axis_index("grp") * share_count, share_count, 0
-    )
-    entry_count = float(sectors * groups * share_count * columns)
-    owned_rows = owner_gather(start_vector) * owner_mask.astype(jnp.bfloat16)
-    first_mixed = contract(owned_rows, got_blocks, got_codes)
-    owner_total = lax.psum(
-        jnp.einsum("wrk,wkn->rn", first_mixed, mixing, preferred_element_type=jnp.float32).astype(
-            jnp.bfloat16
-        ),
-        "grp",
-    ).astype(jnp.float32)
-    owner_first = (owner_total * owner_mask).astype(jnp.bfloat16)
-    first_product = lax.dynamic_slice_in_dim(
-        owner_first, lax.axis_index("grp") * share_count, share_count, 0
-    )
-    widened = first_product.astype(jnp.float32)
-    squares = lax.psum(jnp.sum(widened * widened), ("sector", "grp"))
-    inverse_norm = lax.rsqrt(squares / entry_count + epsilon)
-    second_mixed = contract(owner_first, got_blocks, got_codes)
-    second_product = (channel_share(second_mixed, mixing) * inverse_norm * share_mask).astype(jnp.bfloat16)
-    return (first_product, second_product)
+    return tuple(two_products(assemble(got_blocks, got_codes), mixing, owned_rows, owner_mask))
 
 
 def solution(mesh):

time: 514 us -> 185 us (0.36)
  the two profiles are of different devices: /device:TPU:4 before, /device:TPU:50 now
where the time goes in v1:
time: 185 us; the launch traced here: 184 us
  Pallas kernels  102 us (55%)
  local copies, waits for them, and re-layouts  59.1 us (32%)
  starting transfers between devices  14.5 us (8%)
  other arithmetic  4.65 us (3%)
  matrix products  3.75 us (2%)
    pallas_call x1, Pallas kernels, two_products(): pl.pallas_call(functools.partial(step_kernel, chips, sectors), out_shape=...  66.2 us
    pallas_call x1, Pallas kernels, gather_all(): pl.pallas_call(functools.partial(gather_kernel, chips), out_shape=[jax.Sh...  35.4 us
    reshape x2, local copies, waits for them, and re-layouts, local(): right_site.reshape(WM, WM, D1, D1)  17.2 us
    reshape x2, local copies, waits for them, and re-layouts, local(): mixing.reshape(channels, PHYS, PHYS, RB, RB).transpose(0, 2, 3, 1, 4)  13.4 us
    reshape x2, local copies, waits for them, and re-layouts, local(): packed.reshape(channels, sectors, CAP, TR * TR)  8.14 us
    all_to_all x1, starting transfers between devices, local(): lax.all_to_all(slot_codes.reshape(channels, sectors, CAP), 'sector', spli...  7.25 us
    all_to_all x1, starting transfers between devices, local(): lax.all_to_all(packed.reshape(channels, sectors, CAP, TR * TR), 'sector',...  7.23 us
    reshape x1, local copies, waits for them, and re-layouts, local(): mixing = mixing.reshape(channels, PHYS, PHYS, RB, RB).transpose(0, 2, 3,...  5.94 us
  transfers between devices with their start and end apart: 2, of which 0 were waited for; matrix products, arithmetic and copies ran while one was open for 29% of the time, Pallas kernels for 19%

profile of v1, /device:TPU:50, one launch (start us, length us, event | category | flops | bytes accessed | tf_op | source)
XLA Modules:
  0.0 184.4 jit_solution(6915017204679074831)
XLA Ops:
  0.6 0.8 fusion.4
  1.4 0.9 select_reduce_fusion.1
  2.3 0.7 fusion.15
  3.0 0.7 add_add_fusion
  3.9 0.6 copy.28
  4.5 7.3 %all-to-all-start = ((s32[2,16,2]{2,0,1:T(2,128)}), s32[2,16,2]{2,0,1:T(2,128)S(1)}, u32[]{:S(2)}, u32[]{:S(2)}) async-start(s32[2,16,2]{2,0,1:T(2,128)} %copy.28), calls=%async_computation | async-start | bytes 32768 | tf_op jit(solution)/shard_map/all_to_all | solution.py:452
  11.7 3.7 %reshape.106 = bf16[2,24,16384]{2,1,0:T(8,128)(2,1)} reshape(bf16[2,24,128,128]{3,2,1,0:T(8,128)(2,1)} %param.12) | data formatting | bytes 3145728 | tf_op jit(solution)/shard_map/reshape | solution.py:438
  15.4 2.2 %convolution_convert_fusion = bf16[2,32,16384]{2,1,0:T(8,128)(2,1)S(1)} fusion(bf16[2,24,16384]{2,1,0:T(8,128)(2,1)} %reshape.106, s32[2,24]{1,0:T(2,128)S(1)} %fusion.15), kind=kOutput, calls=%fused_computation | convolution fusion | flops 51381760 | bytes 3670208 | tf_op jit(solution)/shard_map/wes,wen->wsn/dot_general | solution.py:435
  17.7 2.7 %reshape.107 = bf16[2,16,2,16384]{3,2,1,0:T(2,128)(2,1)} reshape(bf16[2,32,16384]{2,1,0:T(8,128)(2,1)S(1)} %convolution_convert_fusion) | data formatting | bytes 4194304 | tf_op jit(solution)/shard_map/reshape | solution.py:446
  20.3 5.5 %copy.29 = bf16[2,16,2,16384]{3,2,0,1:T(2,128)(2,1)} copy(bf16[2,16,2,16384]{3,2,1,0:T(2,128)(2,1)} %reshape.107) | data formatting | bytes 4194304 | tf_op jit(solution)/shard_map/reshape | solution.py:446
  25.8 7.2 %all-to-all-start.1 = ((bf16[2,16,2,16384]{3,2,0,1:T(2,128)(2,1)}), bf16[2,16,2,16384]{3,2,0,1:T(2,128)(2,1)S(1)}, u32[]{:S(2)}, u32[]{:S(2)}) async-start(bf16[2,16,2,16384]{3,2,0,1:T(2,128)(2,1)} %copy.29), calls=%async_computation.1 | async-start | bytes 4194304 | tf_op jit(solution)/shard_map/all_to_all | solution.py:445
  33.0 35.4 %shard_map.113 = (bf16[16,2,16,512]{3,2,1,0:T(8,128)(2,1)}, bf16[16,2,2,1024]{3,2,1,0:T(2,128)(2,1)}, bf16[16,2,2,1024]{3,2,1,0:T(2,128)(2,1)}) custom-call(bf16[16,512]{1,0:T(8,128)(2,1)} %rows_ref.1, bf16[2,1024]{1,0:T(2,128)(2,1)} %site_ref.1, bf16[2,1024]{1,0:T(2,128)(2,1)} %env_ref.1), custom_call_target="tpu_custom_call" | custom-call | tf_op jit(solution)/shard_map/pallas_call | solution.py:166
  68.4 10.8 %reshape.110 = bf16[64,64,4,4]{3,2,1,0:T(4,128)(2,1)} reshape(bf16[16,2,2,1024]{3,2,1,0:T(2,128)(2,1)} %get-tuple-element.5) | data formatting | bytes 262144 | tf_op jit(solution)/shard_map/reshape | solution.py:414
  79.2 6.4 %copy.38 = bf16[64,64,4,4,1,1]{1,0,5,4,3,2:T(8,128)(2,1)S(1)} copy(bf16[64,64,4,4,1,1]{3,2,1,0,5,4:T(4,128)(2,1)} %bitcast.46) | data formatting | bytes 262144 | tf_op jit(solution)/shard_map/reshape | solution.py:414
  87.2 4.4 %reshape.113 = bf16[2,16,16,32,32]{4,3,2,1,0:T(8,128)(2,1)} reshape(bf16[2,256,1024]{2,1,0:T(8,128)(2,1)S(1)} %convolution_convert_fusion.3) | data formatting | bytes 2097152 | tf_op jit(solution)/shard_map/reshape | solution.py:424
  91.6 9.0 %copy.52 = bf16[2,16,16,32,32]{4,1,3,2,0:T(8,128)(2,1)} copy(bf16[2,16,16,32,32]{4,3,2,1,0:T(8,128)(2,1)} %reshape.113) | data formatting | bytes 2097152 | tf_op jit(solution)/shard_map/reshape | solution.py:424
  100.6 5.9 %reshape.114.mix_ref = bf16[2,512,512]{2,1,0:T(8,128)(2,1)S(1)} reshape(bf16[2,16,32,16,32]{4,3,2,1,0:T(8,128)(2,1)} %bitcast.45) | data formatting | bytes 2097152 | tf_op jit(solution)/shard_map/reshape | solution.py:426
  107.3 2.6 %fusion.16 = (bf16[1,16,2,16384]{3,2,0,1:T(2,128)(2,1)}, bf16[1,16,2,16384]{3,2,0,1:T(2,128)(2,1)}) fusion(bf16[2,16,2,16384]{3,2,0,1:T(2,128)(2,1)S(1)} %all-to-all-done.1), kind=kLoop, calls=%fused_computation.36 | loop fusion | bytes 4194304 | tf_op jit(solution)/shard_map/slice | solution.py:374
  109.9 1.5 reshape_squeeze.8
  112.3 1.0 stack_reshape.6
  114.7 1.0 stack_reshape.7
  115.7 1.3 pad_maximum_fusion.dense_ref
  117.0 66.2 %shard_map.114 = (bf16[16,512]{1,0:T(8,128)(2,1)S(1)}, bf16[16,512]{1,0:T(8,128)(2,1)S(1)}) custom-call(bf16[2,512,512]{2,1,0:T(8,128)(2,1)S(1)} %pad_maximum_fusion.dense_ref, bf16[2,512,512]{2,1,0:T(8,128)(2,1)S(1)} %reshape.114.mix_ref, bf16[16,2,16,512]{3,2,1,0:T(8,128)(2,1)S(1)} %copy-done, f32[512,1]{1,0:T(8,128)S(1)} %copy.37.mask_ref), custom_call_target="tpu_custom_call" | custom-call | tf_op jit(solution)/shard_map/pallas_call | solution.py:342
  183.2 0.6 copy.57
  (42 shorter events, 5.3 us)
Async XLA Ops:
  4.5 21.3 %all-to-all-start = ((s32[2,16,2]{2,0,1:T(2,128)}), s32[2,16,2]{2,0,1:T(2,128)S(1)}, u32[]{:S(2)}, u32[]{:S(2)}) async-start(s32[2,16,2]{2,0,1:T(2,128)} %copy.28), calls=%async_computation | async-start | bytes 32768 | tf_op jit(solution)/shard_map/all_to_all | solution.py:452
  25.8 81.5 %all-to-all-start.1 = ((bf16[2,16,2,16384]{3,2,0,1:T(2,128)(2,1)}), bf16[2,16,2,16384]{3,2,0,1:T(2,128)(2,1)S(1)}, u32[]{:S(2)}, u32[]{:S(2)}) async-start(bf16[2,16,2,16384]{3,2,0,1:T(2,128)(2,1)} %copy.29), calls=%async_computation.1 | async-start | bytes 4194304 | tf_op jit(solution)/shard_map/all_to_all | solution.py:445
  79.2 6.5 %copy-start.5 = (s32[2,64]{1,0:T(2,128)S(1)}, s32[2,64]{1,0:T(2,128)}, u32[]{:S(2)}) copy-start(s32[2,64]{1,0:T(2,128)} %param.17) | copy-start | bytes 1540
  79.2 6.9 %copy-start.3 = (bf16[2,1024]{1,0:T(2,128)(2,1)S(1)}, bf16[2,1024]{1,0:T(2,128)(2,1)}, u32[]{:S(2)}) copy-start(bf16[2,1024]{1,0:T(2,128)(2,1)} %param.16) | copy-start | bytes 12292
  79.2 7.5 %copy-start.2 = (bf16[16,2,2,1024]{3,2,1,0:T(2,128)(2,1)S(1)}, bf16[16,2,2,1024]{3,2,1,0:T(2,128)(2,1)}, u32[]{:S(2)}) copy-start(bf16[16,2,2,1024]{3,2,1,0:T(2,128)(2,1)} %get-tuple-element.6) | copy-start | bytes 393220
  100.6 6.0 %copy-start.4 = (s32[4]{0:T(128)S(1)}, s32[4]{0:T(128)}, u32[]{:S(2)}) copy-start(s32[4]{0:T(128)} %param.11) | copy-start | bytes 52
  111.4 2.0 %copy-start.1 = (bf16[1,16,2,16384]{3,2,0,1:T(2,128)(2,1)S(1)}, bf16[1,16,2,16384]{3,2,0,1:T(2,128)(2,1)}, u32[]{:S(2)}) copy-start(bf16[1,16,2,16384]{3,2,0,1:T(2,128)(2,1)} %get-tuple-element.13) | copy-start | bytes 3145732
  114.3 2.7 %copy-start = (bf16[16,2,16,512]{3,2,1,0:T(8,128)(2,1)S(1)}, bf16[16,2,16,512]{3,2,1,0:T(8,128)(2,1)}, u32[]{:S(2)}) copy-start(bf16[16,2,16,512]{3,2,1,0:T(8,128)(2,1)} %get-tuple-element.7.start_ref) | copy-start | bytes 1572868

commit v2 on v1

--- a/solution.py
+++ b/solution.py
@@ -366,25 +366,127 @@
     )(dense, mixing, owned_rows, owner_mask)
 
 
-def assemble(got_blocks, got_codes):
-    channels = got_blocks.shape[0]
-    slot_count = got_blocks.shape[1] * got_blocks.shape[2]
-    results = []
+def pack_kernel(pick_ref, env_ref, out_ref):
+    def one_slot(slot, carry):
+        pick = pick_ref[slot]
+
+        @pl.when(pick > 0)
+        def _():
+            out_ref[slot] = env_ref[pick - 1]
+
+        @pl.when(pick <= 0)
+        def _():
+            out_ref[slot] = jnp.zeros_like(out_ref[slot])
+
+        return carry
+
+    lax.fori_loop(0, out_ref.shape[0], one_slot, 0)
+
+
+def pack(pick, blocks):
+    return pl.pallas_call(
+        pack_kernel,
+        out_shape=jax.ShapeDtypeStruct((pick.shape[0], TR, TR), blocks.dtype),
+        in_specs=[
+            pl.BlockSpec(memory_space=pltpu.SMEM),
+            pl.BlockSpec(memory_space=pltpu.VMEM),
+        ],
+        out_specs=pl.BlockSpec(memory_space=pltpu.VMEM),
+    )(pick, blocks)
+
+
+def assemble_kernel(code_ref, blocks_ref, out_ref, total):
+    total[...] = jnp.zeros_like(total)
+    channels = out_ref.shape[0]
+
+    def one_slot(slot, carry):
+        code = code_ref[slot]
+        channel = lax.rem(slot // CAP, channels)
+
+        @pl.when(code > 0)
+        def _():
+            place = channel * TPO * TPO + code - 1
+            total[place] = total[place] + blocks_ref[slot].astype(jnp.float32)
+
+        return carry
+
+    lax.fori_loop(0, blocks_ref.shape[0], one_slot, 0)
     for channel in range(channels):
-        blocks = got_blocks[channel].reshape(slot_count, TR * TR)
-        slot_codes = got_codes[channel].reshape(slot_count)
-        tile_index = jnp.maximum(slot_codes - 1, 0)
-        pair_hot = (
-            (tile_index[:, None] == jnp.arange(TPO * TPO, dtype=jnp.int32)[None, :])
-            & (slot_codes[:, None] > 0)
+        for row in range(TPO):
+            for col in range(TPO):
+                out_ref[channel, row * TR : (row + 1) * TR, col * TR : (col + 1) * TR] = total[
+                    (channel * TPO + row) * TPO + col
+                ].astype(out_ref.dtype)
+
+
+def assemble(codes, blocks, channels):
+    return pl.pallas_call(
+        assemble_kernel,
+        out_shape=jax.ShapeDtypeStruct((channels, TPO * TR, TPO * TR), jnp.bfloat16),
+        in_specs=[
+            pl.BlockSpec(memory_space=pltpu.SMEM),
+            pl.BlockSpec(memory_space=pltpu.VMEM),
+        ],
+        out_specs=pl.BlockSpec(memory_space=pltpu.VMEM),
+        scratch_shapes=[pltpu.VMEM((channels * TPO * TPO, TR, TR), jnp.float32)],
+    )(codes, blocks)
+
+
+def mixing_kernel(left_ref, site_ref, env_ref, out_ref, wide):
+    group = D1 * WM
+    joined = jnp.concatenate(
+        [
+            jnp.dot(
+                left_ref[...],
+                site_ref[:, d * group : (d + 1) * group],
+                preferred_element_type=jnp.float32,
+            )
+            for d in range(D1)
+        ],
+        axis=0,
+    ).astype(jnp.bfloat16)
+    lanes = D1 * RB
+    held = out_ref.shape[0] * D1
+    source = lax.broadcasted_iota(jnp.int32, (lanes, D1 * lanes), 0)
+    column = lax.broadcasted_iota(jnp.int32, (lanes, D1 * lanes), 1)
+    repeat = jnp.where(
+        source == (column // lanes) * RB + lax.rem(column, RB), 1.0, 0.0
+    ).astype(jnp.bfloat16)
+    piece = lax.rem(lax.broadcasted_iota(jnp.int32, (WM, D1 * lanes), 1), lanes) // RB
+    for tile in range(RB // D1):
+        spread_env = jnp.dot(
+            env_ref[:, tile * lanes : (tile + 1) * lanes],
+            repeat,
+            preferred_element_type=jnp.float32,
+        )
+        stacked = jnp.concatenate(
+            [jnp.where(piece == b, spread_env, 0.0) for b in range(D1)], axis=0
         ).astype(jnp.bfloat16)
-        summed = jnp.einsum(
-            "sp,sq->pq", pair_hot, blocks, preferred_element_type=jnp.float32
-        ).astype(jnp.bfloat16)
-        results.append(
-            summed.reshape(TPO, TPO, TR, TR).transpose(0, 2, 1, 3).reshape(TPO * TR, TPO * TR)
-        )
-    return jnp.stack(results)
+        result = jnp.dot(joined, stacked, preferred_element_type=jnp.float32)
+        for d in range(D1):
+            for a in range(D1):
+                at = (d * D1 + a) * held
+                for k in range(D1):
+                    wide[:, d * RB + tile * D1 + k, a * lanes : (a + 1) * lanes] = result[
+                        at : at + held, k * lanes : (k + 1) * lanes
+                    ]
+    for channel in range(out_ref.shape[0]):
+        out_ref[channel] = (
+            wide[channel * D1 : (channel + 1) * D1]
+            .reshape(out_ref.shape[1], out_ref.shape[2])
+            .astype(out_ref.dtype)
+        )
+
+
+def build_mixing(left, site, env, channels):
+    columns = PHYS * RB
+    return pl.pallas_call(
+        mixing_kernel,
+        out_shape=jax.ShapeDtypeStruct((channels, columns, columns), jnp.bfloat16),
+        in_specs=[pl.BlockSpec(memory_space=pltpu.VMEM)] * 3,
+        out_specs=pl.BlockSpec(memory_space=pltpu.VMEM),
+        scratch_shapes=[pltpu.VMEM((channels * D1, D1 * RB, columns), jnp.float32)],
+    )(left, site, env)
 
 
 def local(
@@ -400,30 +502,18 @@
     right_env,
 ):
     sectors = lax.axis_size("sector")
-    columns = start_vector.shape[1]
     channels = env_blocks.shape[0]
     held_blocks = env_blocks.shape[1]
-    owned_rows, right_site, right_panels = gather_all(start_vector, site_right, right_env)
-    right_panels = right_panels.reshape(WM, RB * RB)
+    site_local = (
+        site_right.reshape(channels, WM, D1, D1).transpose(0, 3, 2, 1).reshape(channels, WM * PHYS)
+    )
     left_site = (
         site_left.reshape(channels, WM, D1, D1) * mpo_pattern.astype(jnp.bfloat16)[:, :, None, None]
     )
-    joined = jnp.einsum(
-        "wmac,mxbd->wxabcd",
-        left_site,
-        right_site.reshape(WM, WM, D1, D1),
-        preferred_element_type=jnp.float32,
-    ).astype(jnp.bfloat16)
-    mixing = jnp.einsum(
-        "wxq,xr->wqr",
-        joined.reshape(channels, WM, PHYS * PHYS),
-        right_panels,
-        preferred_element_type=jnp.float32,
-    ).astype(jnp.bfloat16)
-    mixing = (
-        mixing.reshape(channels, PHYS, PHYS, RB, RB)
-        .transpose(0, 2, 3, 1, 4)
-        .reshape(channels, columns, columns)
+    left_rows = left_site.transpose(2, 0, 3, 1).reshape(D1 * channels * D1, WM)
+    owned_rows, site_all, env_all = gather_all(start_vector, site_local, right_env)
+    mixing = build_mixing(
+        left_rows, site_all.reshape(WM, WM * PHYS), env_all.reshape(WM, RB * RB), channels
     )
     owners = block_owner[:, :, 0]
     owner_hot = (owners[:, :, None] == jnp.arange(sectors, dtype=jnp.int32)[None, None, :]).astype(
@@ -432,34 +522,38 @@
     position = jnp.sum((jnp.cumsum(owner_hot, axis=1) - owner_hot) * owner_hot, axis=2)
     slot_index = owners * CAP + position
     select = slot_index[:, :, None] == jnp.arange(sectors * CAP, dtype=jnp.int32)[None, None, :]
-    packed = jnp.einsum(
-        "wes,wen->wsn",
-        select.astype(jnp.bfloat16),
-        env_blocks.reshape(channels, held_blocks, TR * TR),
-        preferred_element_type=jnp.float32,
-    ).astype(jnp.bfloat16)
-    slot_codes = jnp.sum(
-        select.astype(jnp.int32) * (1 + block_rows * TPO + block_cols)[:, :, None], axis=1
-    )
-    got_blocks, got_codes = (
-        lax.all_to_all(
-            packed.reshape(channels, sectors, CAP, TR * TR),
-            "sector",
-            split_axis=1,
-            concat_axis=1,
-            tiled=True,
-        ),
-        lax.all_to_all(
-            slot_codes.reshape(channels, sectors, CAP),
-            "sector",
-            split_axis=1,
-            concat_axis=1,
-            tiled=True,
-        ),
+    chosen = select.astype(jnp.int32)
+
+    def by_owner(values):
+        return values.reshape(channels, sectors, CAP).transpose(1, 0, 2)
+
+    block_number = jnp.arange(1, 1 + channels * held_blocks, dtype=jnp.int32)
+    pick = by_owner(
+        jnp.sum(chosen * block_number.reshape(channels, held_blocks)[:, :, None], axis=1)
+    )
+    slot_codes = by_owner(
+        jnp.sum(chosen * (1 + block_rows * TPO + block_cols)[:, :, None], axis=1)
+    )
+    slots = channels * CAP
+    packed = pack(
+        pick.reshape(sectors * slots), env_blocks.reshape(channels * held_blocks, TR, TR)
+    )
+    got_codes = lax.all_to_all(
+        slot_codes.reshape(sectors, slots), "sector", split_axis=0, concat_axis=0, tiled=True
+    )
+    got_blocks = lax.all_to_all(
+        packed.reshape(sectors, slots, TR, TR),
+        "sector",
+        split_axis=0,
+        concat_axis=0,
+        tiled=True,
+    )
+    dense = assemble(
+        got_codes.reshape(sectors * slots), got_blocks.reshape(sectors * slots, TR, TR), channels
     )
     tile_mask = (jnp.arange(TR, dtype=jnp.int32)[None, :] < tile_live[:, None]).reshape(TPO * TR)
     owner_mask = tile_mask.astype(jnp.float32)[:, None]
-    return tuple(two_products(assemble(got_blocks, got_codes), mixing, owned_rows, owner_mask))
+    return tuple(two_products(dense, mixing, owned_rows, owner_mask))
 
 
 def solution(mesh):

time: 185 us -> 145 us (0.78)
  the two profiles are of different devices: /device:TPU:50 before, /device:TPU:52 now
where the time goes in v2:
time: 145 us
  Pallas kernels  115 us (79%)
  starting transfers between devices  14.6 us (10%)
  local copies, waits for them, and re-layouts  10.7 us (7%)
  other arithmetic  4.1 us (3%)
    pallas_call x1, Pallas kernels, two_products(): pl.pallas_call(functools.partial(step_kernel, chips, sectors), out_shape=...  66.1 us
    pallas_call x1, Pallas kernels, gather_all(): pl.pallas_call(functools.partial(gather_kernel, chips), out_shape=[jax.Sh...  35.3 us
    all_to_all x1, starting transfers between devices, local(): lax.all_to_all(packed.reshape(sectors, slots, TR, TR), 'sector', split_ax...  7.37 us
    all_to_all x1, starting transfers between devices, local(): lax.all_to_all(slot_codes.reshape(sectors, slots), 'sector', split_axis=0...  7.23 us
    pallas_call x1, Pallas kernels, build_mixing(): pl.pallas_call(mixing_kernel, out_shape=jax.ShapeDtypeStruct((channels, c...  4.82 us
    pallas_call x1, Pallas kernels, assemble(): pl.pallas_call(assemble_kernel, out_shape=jax.ShapeDtypeStruct((channels,...  4.38 us
    pallas_call x1, Pallas kernels, pack(): pl.pallas_call(pack_kernel, out_shape=jax.ShapeDtypeStruct((pick.shape[0]...  3.98 us
  transfers between devices with their start and end apart: 2, of which 0 were waited for; matrix products, arithmetic and copies ran while one was open for 6% of the time, Pallas kernels for 30%

profile of v2, /device:TPU:52, one launch (start us, length us, event | category | flops | bytes accessed | tf_op | source)
XLA Modules:
  0.0 144.8 jit_solution(8701622406319723981)
XLA Ops:
  0.6 0.8 fusion
  1.4 0.9 select_reduce_fusion.2
  2.3 0.7 add_add_fusion
  3.0 0.7 fusion.2
  4.0 0.7 copy.34
  4.7 7.2 %all-to-all-start = ((s32[16,1,4]{2,1,0:T(1,128)}), s32[16,1,4]{2,1,0:T(1,128)S(1)}, u32[]{:S(2)}, u32[]{:S(2)}) async-start(s32[16,1,4]{2,1,0:T(1,128)} %copy.34), calls=%async_computation | async-start | bytes 16384 | tf_op jit(solution)/shard_map/all_to_all | solution.py:541
  12.0 0.6 reshape.89.pick_ref
  12.6 4.0 %shard_map.113 = bf16[64,128,128]{2,1,0:T(8,128)(2,1)} custom-call(s32[64]{0:T(128)} %reshape.89.pick_ref, bf16[48,128,128]{2,1,0:T(8,128)(2,1)} %bitcast.20), custom_call_target="tpu_custom_call" | custom-call | tf_op jit(solution)/shard_map/pallas_call | solution.py:387
  16.6 7.4 %all-to-all-start.1 = ((bf16[16,4,128,128]{3,2,1,0:T(8,128)(2,1)}), bf16[16,4,128,128]{3,2,1,0:T(8,128)(2,1)}, u32[]{:S(2)}, u32[]{:S(2)}) async-start(bf16[16,4,128,128]{3,2,1,0:T(8,128)(2,1)} %bitcast.19), calls=%async_computation.1 | async-start | bytes 4194304 | tf_op jit(solution)/shard_map/all_to_all | solution.py:544
  24.0 0.3 reshape.93
  24.5 0.7 copy.36
  25.7 0.7 reshape.96.site_ref
  26.4 35.3 %shard_map.115 = (bf16[16,2,16,512]{3,2,1,0:T(8,128)(2,1)}, bf16[16,2,2,1024]{3,2,1,0:T(2,128)(2,1)}, bf16[16,2,2,1024]{3,2,1,0:T(2,128)(2,1)}) custom-call(bf16[16,512]{1,0:T(8,128)(2,1)} %rows_ref.1, bf16[2,1024]{1,0:T(2,128)(2,1)} %reshape.96.site_ref, bf16[2,1024]{1,0:T(2,128)(2,1)} %env_ref.1), custom_call_target="tpu_custom_call" | custom-call | tf_op jit(solution)/shard_map/pallas_call | solution.py:166
  61.7 1.6 %reshape.97.site_ref = bf16[64,1024]{1,0:T(8,128)(2,1)} reshape(bf16[16,2,2,1024]{3,2,1,0:T(2,128)(2,1)} %get-tuple-element.5) | data formatting | bytes 262144 | tf_op jit(solution)/shard_map/reshape | solution.py:516
  63.4 1.6 %reshape.98.env_ref = bf16[64,1024]{1,0:T(8,128)(2,1)} reshape(bf16[16,2,2,1024]{3,2,1,0:T(2,128)(2,1)} %get-tuple-element.6) | data formatting | bytes 262144 | tf_op jit(solution)/shard_map/reshape | solution.py:516
  65.2 4.8 %shard_map.116.mix_ref = bf16[2,512,512]{2,1,0:T(8,128)(2,1)} custom-call(bf16[32,64]{1,0:T(8,128)(2,1)} %bitcast.24, bf16[64,1024]{1,0:T(8,128)(2,1)} %reshape.97.site_ref, bf16[64,1024]{1,0:T(8,128)(2,1)} %reshape.98.env_ref), custom_call_target="tpu_custom_call" | custom-call | tf_op jit(solution)/shard_map/pallas_call | solution.py:483
  70.0 0.5 broadcast.30
  70.5 0.7 reduce.3
  71.2 0.6 reshape.87.code_ref
  71.8 4.4 %shard_map.114.dense_ref = bf16[2,512,512]{2,1,0:T(8,128)(2,1)} custom-call(s32[64]{0:T(128)} %reshape.87.code_ref, bf16[64,128,128]{2,1,0:T(8,128)(2,1)} %bitcast.9.blocks_ref), custom_call_target="tpu_custom_call" | custom-call | tf_op jit(solution)/shard_map/pallas_call | solution.py:423
  76.2 1.2 copy-done.1
  77.4 66.1 %shard_map.117 = (bf16[16,512]{1,0:T(8,128)(2,1)S(1)}, bf16[16,512]{1,0:T(8,128)(2,1)S(1)}) custom-call(bf16[2,512,512]{2,1,0:T(8,128)(2,1)S(1)} %copy-done.1, bf16[2,512,512]{2,1,0:T(8,128)(2,1)S(1)} %copy-done, bf16[16,2,16,512]{3,2,1,0:T(8,128)(2,1)S(1)} %copy-done.2, f32[512,1]{1,0:T(8,128)S(1)} %copy.38.mask_ref), custom_call_target="tpu_custom_call" | custom-call | tf_op jit(solution)/shard_map/pallas_call | solution.py:342
  143.5 0.6 copy.41
  144.2 0.6 copy.42
  (27 shorter events, 1.3 us)
Async XLA Ops:
  4.7 11.9 %all-to-all-start = ((s32[16,1,4]{2,1,0:T(1,128)}), s32[16,1,4]{2,1,0:T(1,128)S(1)}, u32[]{:S(2)}, u32[]{:S(2)}) async-start(s32[16,1,4]{2,1,0:T(1,128)} %copy.34), calls=%async_computation | async-start | bytes 16384 | tf_op jit(solution)/shard_map/all_to_all | solution.py:541
  16.6 7.4 %copy-start.3 = (bf16[2,1024]{1,0:T(2,128)(2,1)S(1)}, bf16[2,1024]{1,0:T(2,128)(2,1)}, u32[]{:S(2)}) copy-start(bf16[2,1024]{1,0:T(2,128)(2,1)} %param.16) | copy-start | bytes 12292
  16.6 7.7 %copy-start.6 = (s32[2,64]{1,0:T(2,128)S(1)}, s32[2,64]{1,0:T(2,128)}, u32[]{:S(2)}) copy-start(s32[2,64]{1,0:T(2,128)} %param.17) | copy-start | bytes 1540
  16.6 8.7 %copy-start.4 = (bf16[2,1024]{1,0:T(2,128)(2,1)S(1)}, bf16[2,1024]{1,0:T(2,128)(2,1)}, u32[]{:S(2)}) copy-start(bf16[2,1024]{1,0:T(2,128)(2,1)} %param.18) | copy-start | bytes 12292
  16.6 48.4 %copy-start.5 = (s32[4]{0:T(128)S(1)}, s32[4]{0:T(128)}, u32[]{:S(2)}) copy-start(s32[4]{0:T(128)} %param.11) | copy-start | bytes 52
  16.6 55.2 %all-to-all-start.1 = ((bf16[16,4,128,128]{3,2,1,0:T(8,128)(2,1)}), bf16[16,4,128,128]{3,2,1,0:T(8,128)(2,1)}, u32[]{:S(2)}, u32[]{:S(2)}) async-start(bf16[16,4,128,128]{3,2,1,0:T(8,128)(2,1)} %bitcast.19), calls=%async_computation.1 | async-start | bytes 4194304 | tf_op jit(solution)/shard_map/all_to_all | solution.py:544
  65.2 11.0 %copy-start.2 = (bf16[16,2,16,512]{3,2,1,0:T(8,128)(2,1)S(1)}, bf16[16,2,16,512]{3,2,1,0:T(8,128)(2,1)}, u32[]{:S(2)}) copy-start(bf16[16,2,16,512]{3,2,1,0:T(8,128)(2,1)} %get-tuple-element.7.start_ref) | copy-start | bytes 1572868
  70.0 6.2 %copy-start = (bf16[2,512,512]{2,1,0:T(8,128)(2,1)S(1)}, bf16[2,512,512]{2,1,0:T(8,128)(2,1)}, u32[]{:S(2)}) copy-start(bf16[2,512,512]{2,1,0:T(8,128)(2,1)} %shard_map.116.mix_ref) | copy-start | bytes 3145732
  76.2 1.2 copy-start.1

commit v3 on v2

--- a/solution.py
+++ b/solution.py
@@ -66,111 +66,168 @@
         pl.semaphore_wait(barrier, chips)
 
 
-def spread(held, chips, chip, core, send_sem, recv_sem, pair_send, pair_recv):
+NEAR = 4
+
+
+def offsets(core):
+    return (1, -1, 2 - 4 * core)
+
+
+def spread(items, chips, chip, core, sems):
+    far_count = chips // NEAR
     sibling = {"grp": chip * 2 + 1 - core}
-    mine = held.at[chip, core]
-
-    def outgoing(step):
-        other = lax.rem(chip + step, chips)
-        return send_to(
-            mine, mine, send_sem.at[step], recv_sem.at[step], {"grp": other * 2 + core}
-        )
-
-    def forward(step):
-        source = lax.rem(chip + chips - step, chips)
-        block = held.at[source, core]
-        return send_to(block, block, pair_send.at[step], pair_recv.at[step], sibling)
-
-    def start(step, carry):
-        outgoing(step).start()
-        return carry
-
-    def relay(step, carry):
-        outgoing(step).wait_recv()
-        forward(step).start()
-        return carry
-
-    def finish(step, carry):
-        outgoing(step).wait_send()
-        return carry
-
-    def finish_pair(step, carry):
-        forward(step).wait()
-        return carry
-
-    lax.fori_loop(1, chips, start, 0)
-    forward(0).start()
-    lax.fori_loop(1, chips, relay, 0)
-    lax.fori_loop(1, chips, finish, 0)
-    lax.fori_loop(0, chips, finish_pair, 0)
-
-
-def gather_kernel(chips, rows_ref, site_ref, env_ref, rows_out, site_out, env_out, *sems):
-    position = lax.axis_index("grp")
-    chip, core = position // 2, lax.rem(position, 2)
     send_sem, recv_sem, pair_send, pair_recv = sems
-    pairs = ((rows_ref, rows_out), (site_ref, site_out), (env_ref, env_out))
-    for source, target in pairs:
-        target[chip, core] = source[...]
-    greet(chips, chip, core)
-    sibling = {"grp": chip * 2 + 1 - core}
-
-    def outgoing(item, step):
-        other = lax.rem(chip + step, chips)
-        mine = pairs[item][1].at[chip, core]
+    numbers = range(len(items))
+
+    def far(item, step):
+        mine = items[item].at[chip, core]
+        target = lax.rem(chip + step * NEAR, chips)
         return send_to(
             mine,
             mine,
             send_sem.at[item, step],
             recv_sem.at[item, step],
-            {"grp": other * 2 + core},
-        )
-
-    def forward(item, step):
-        source = lax.rem(chip + chips - step, chips)
-        block = pairs[item][1].at[source, core]
-        return send_to(block, block, pair_send.at[item, step], pair_recv.at[item, step], sibling)
-
-    def start(step, carry):
-        for item in (1, 2, 0):
-            outgoing(item, step).start()
-        return carry
-
-    def relay(step, carry):
-        for item in (1, 2, 0):
-            outgoing(item, step).wait_recv()
-            forward(item, step).start()
-        return carry
-
-    def finish(step, carry):
-        for item in (1, 2, 0):
-            outgoing(item, step).wait_send()
-        return carry
-
-    def finish_pair(step, carry):
-        for item in (1, 2, 0):
-            forward(item, step).wait()
-        return carry
-
-    lax.fori_loop(1, chips, start, 0)
-    for item in (1, 2, 0):
-        forward(item, 0).start()
-    lax.fori_loop(1, chips, relay, 0)
-    lax.fori_loop(1, chips, finish, 0)
-    lax.fori_loop(0, chips, finish_pair, 0)
-
-
-def gather_all(start_vector, site_right, right_env):
+            {"grp": target * 2 + core},
+        )
+
+    def near(item, way, step):
+        source = lax.rem(chip + chips - step * NEAR, chips)
+        block = items[item].at[source, core]
+        target = lax.rem(chip + chips + offsets(core)[way], chips)
+        index = (way + 1) * far_count + step
+        return send_to(
+            block,
+            block,
+            send_sem.at[item, index],
+            recv_sem.at[item, index],
+            {"grp": target * 2 + core},
+        )
+
+    def forward(item, source, index):
+        block = items[item].at[source, core]
+        return send_to(
+            block, block, pair_send.at[item, index], pair_recv.at[item, index], sibling
+        )
+
+    def forward_far(item, step):
+        return forward(item, lax.rem(chip + chips - step * NEAR, chips), step)
+
+    def forward_near(item, way, step):
+        source = lax.rem(chip + 2 * chips - offsets(core)[way] - step * NEAR, chips)
+        return forward(item, source, (way + 1) * far_count + step)
+
+    def far_start(step, carry):
+        for item in numbers:
+            far(item, step).start()
+        return carry
+
+    def far_relay(step, carry):
+        for item in numbers:
+            far(item, step).wait_recv()
+            for way in range(NEAR - 1):
+                near(item, way, step).start()
+            forward_far(item, step).start()
+        return carry
+
+    def near_relay(step, carry):
+        for item in numbers:
+            for way in range(NEAR - 1):
+                near(item, way, step).wait_recv()
+                forward_near(item, way, step).start()
+        return carry
+
+    def far_finish(step, carry):
+        for item in numbers:
+            far(item, step).wait_send()
+        return carry
+
+    def near_finish(step, carry):
+        for item in numbers:
+            forward_far(item, step).wait()
+            for way in range(NEAR - 1):
+                near(item, way, step).wait_send()
+                forward_near(item, way, step).wait()
+        return carry
+
+    lax.fori_loop(1, far_count, far_start, 0)
+    for item in numbers:
+        for way in range(NEAR - 1):
+            near(item, way, 0).start()
+        forward_far(item, 0).start()
+    lax.fori_loop(1, far_count, far_relay, 0)
+    lax.fori_loop(0, far_count, near_relay, 0)
+    lax.fori_loop(1, far_count, far_finish, 0)
+    lax.fori_loop(0, far_count, near_finish, 0)
+
+
+def gather_kernel(
+    chips,
+    sectors,
+    rows_ref,
+    site_ref,
+    env_ref,
+    code_ref,
+    rows_out,
+    site_out,
+    env_out,
+    code_out,
+    send_sem,
+    recv_sem,
+    pair_send,
+    pair_recv,
+    code_sems,
+):
+    position = lax.axis_index("grp")
+    owner = lax.axis_index("sector")
+    chip, core = position // 2, lax.rem(position, 2)
+    for source, target in ((rows_ref, rows_out), (site_ref, site_out), (env_ref, env_out)):
+        target[chip, core] = source[...]
+    code_out[owner] = code_ref[owner]
+    greet(chips, chip, core, sectors)
+
+    def code_copy(step):
+        other = lax.rem(owner + step, sectors)
+        return send_to(
+            code_ref.at[other],
+            code_out.at[owner],
+            code_sems.at[0, step],
+            code_sems.at[1, step],
+            {"sector": other},
+        )
+
+    def code_start(step, carry):
+        code_copy(step).start()
+        return carry
+
+    def code_finish(step, carry):
+        code_copy(step).wait()
+        return carry
+
+    lax.fori_loop(1, sectors, code_start, 0)
+    spread(
+        (site_out, env_out, rows_out),
+        chips,
+        chip,
+        core,
+        (send_sem, recv_sem, pair_send, pair_recv),
+    )
+    lax.fori_loop(1, sectors, code_finish, 0)
+
+
+def gather_all(start_vector, site_right, right_env, codes):
     chips = lax.axis_size("grp") // 2
+    sectors = lax.axis_size("sector")
     operands = (start_vector, site_right, right_env)
     return pl.pallas_call(
-        functools.partial(gather_kernel, chips),
-        out_shape=[jax.ShapeDtypeStruct((chips, 2) + a.shape, a.dtype) for a in operands],
-        in_specs=[pl.BlockSpec(memory_space=pltpu.VMEM)] * 3,
-        out_specs=[pl.BlockSpec(memory_space=pltpu.VMEM)] * 3,
-        scratch_shapes=[pltpu.SemaphoreType.DMA((3, chips))] * 4,
+        functools.partial(gather_kernel, chips, sectors),
+        out_shape=[jax.ShapeDtypeStruct((chips, 2) + a.shape, a.dtype) for a in operands]
+        + [jax.ShapeDtypeStruct(codes.shape, codes.dtype)],
+        in_specs=[pl.BlockSpec(memory_space=pltpu.VMEM)] * 4,
+        out_specs=[pl.BlockSpec(memory_space=pltpu.VMEM)] * 4,
+        scratch_shapes=[pltpu.SemaphoreType.DMA((3, chips))] * 4
+        + [pltpu.SemaphoreType.DMA((2, sectors))],
         compiler_params=pltpu.CompilerParams(collective_id=0, has_side_effects=True),
-    )(*operands)
+    )(*operands, codes)
 
 
 def product(dense_ref, mix_ref, vector, part, base):
@@ -184,56 +241,84 @@
                 dense_ref[channel, rows, :], vector, preferred_element_type=jnp.float32
             ).astype(jnp.bfloat16)
             total += jnp.dot(mixed, mix_ref[channel], preferred_element_type=jnp.float32)
-        split = total.astype(jnp.bfloat16).reshape(tile // (2 * SHARE), 2, SHARE, vector.shape[1])
-        chunk = pl.ds(index * (tile // (2 * SHARE)), tile // (2 * SHARE))
-        part[base, chunk] = split[:, 0]
-        part[base + 1, chunk] = split[:, 1]
+        held = tile // (2 * SHARE * NEAR)
+        split = total.astype(jnp.bfloat16).reshape(held, NEAR, 2, SHARE, vector.shape[1])
+        chunk = pl.ds(index * held, held)
+        for kind in range(NEAR):
+            part[base, kind, chunk] = split[:, kind, 0]
+            part[base + 1, kind, chunk] = split[:, kind, 1]
         return carry
 
     lax.fori_loop(0, TPO * TR // tile, one_tile, 0)
 
 
-def reduce_share(chips, chip, core, part, base, sib, ready, got, sems):
-    pair_send, pair_recv, send_sem, recv_sem = sems
-    pair = send_to(
-        part.at[base + 1 - core],
-        sib,
-        pair_send,
-        pair_recv,
-        {"grp": chip * 2 + 1 - core},
-    )
-    pair.start()
-    pair.wait()
-    ready[...] = (part[base + core].astype(jnp.float32) + sib[...].astype(jnp.float32)).astype(
-        jnp.bfloat16
-    )
-
-    def outgoing(step):
-        other = lax.rem(chip + step, chips)
-        return send_to(
-            ready.at[other],
-            got.at[step],
-            send_sem.at[step],
-            recv_sem.at[step],
-            {"grp": other * 2 + core},
-        )
-
-    def start(step, carry):
-        outgoing(step).start()
-        return carry
-
-    def collect(step, total):
-        outgoing(step).wait_recv()
-        return total + got[step].astype(jnp.float32)
-
-    def finish(step, carry):
-        outgoing(step).wait_send()
-        return carry
-
-    lax.fori_loop(1, chips, start, 0)
-    total = lax.fori_loop(1, chips, collect, ready[chip].astype(jnp.float32))
-    lax.fori_loop(1, chips, finish, 0)
-    return total
+def reduce_share(chips, chip, core, part, base, sib, ready, near_got, far_ready, far_got, sems):
+    pair_sems, near_sems, far_sems = sems
+    ways = offsets(core)[::-1]
+    far_count = chips // NEAR
+
+    def kind_of(way):
+        return lax.rem(chip + chips + ways[way], NEAR) if way < NEAR - 1 else lax.rem(chip, NEAR)
+
+    def pair(way):
+        kind = kind_of(way)
+        return send_to(
+            part.at[base + 1 - core, kind],
+            sib.at[kind],
+            pair_sems.at[0, way],
+            pair_sems.at[1, way],
+            {"grp": chip * 2 + 1 - core},
+        )
+
+    def near(way):
+        target = lax.rem(chip + chips + ways[way], chips)
+        return send_to(
+            ready.at[kind_of(way)],
+            near_got.at[way],
+            near_sems.at[0, way],
+            near_sems.at[1, way],
+            {"grp": target * 2 + core},
+        )
+
+    def far(step):
+        target = lax.rem(chip + step * NEAR, chips)
+        return send_to(
+            far_ready.at[target // NEAR],
+            far_got.at[step],
+            far_sems.at[0, step],
+            far_sems.at[1, step],
+            {"grp": target * 2 + core},
+        )
+
+    for way in range(NEAR):
+        pair(way).start()
+    for way in range(NEAR - 1):
+        pair(way).wait_recv()
+        kind = kind_of(way)
+        ready[kind] = (
+            part[base + core, kind].astype(jnp.float32) + sib[kind].astype(jnp.float32)
+        ).astype(jnp.bfloat16)
+        near(way).start()
+    pair(NEAR - 1).wait_recv()
+    kind = kind_of(NEAR - 1)
+    total = part[base + core, kind].astype(jnp.float32) + sib[kind].astype(jnp.float32)
+    for way in range(NEAR - 1):
+        near(way).wait_recv()
+        total += near_got[way].astype(jnp.float32)
+    far_ready[...] = total.astype(jnp.bfloat16)
+    for step in range(1, far_count):
+        far(step).start()
+    share = far_ready[chip // NEAR].astype(jnp.float32)
+    for step in range(1, far_count):
+        far(step).wait_recv()
+        share += far_got[step].astype(jnp.float32)
+    for way in range(NEAR):
+        pair(way).wait_send()
+    for way in range(NEAR - 1):
+        near(way).wait_send()
+    for step in range(1, far_count):
+        far(step).wait_send()
+    return share
 
 
 def step_kernel(
@@ -246,17 +331,17 @@
     first_out,
     second_out,
     part,
-    sib_one,
-    sib_two,
-    ready_one,
-    ready_two,
-    got_one,
-    got_two,
+    sib,
+    ready,
+    near_got,
+    far_ready,
+    far_got,
     held,
     norm_mine,
     norm_got,
     pair_sems,
-    share_sems,
+    near_sems,
+    far_sems,
     spread_sems,
     norm_sems,
 ):
@@ -275,24 +360,17 @@
         core,
         part,
         0,
-        sib_one,
-        ready_one,
-        got_one,
-        (pair_sems.at[0], pair_sems.at[1], share_sems.at[0], share_sems.at[1]),
+        sib.at[0],
+        ready.at[0],
+        near_got.at[0],
+        far_ready.at[0],
+        far_got.at[0],
+        (pair_sems.at[0], near_sems.at[0], far_sems.at[0]),
     )
     first = (total * share_mask).astype(jnp.bfloat16)
     first_out[...] = first
     held[chip, core] = first
-    spread(
-        held,
-        chips,
-        chip,
-        core,
-        spread_sems.at[0],
-        spread_sems.at[1],
-        spread_sems.at[2],
-        spread_sems.at[3],
-    )
+    spread((held,), chips, chip, core, [spread_sems.at[at] for at in range(4)])
     wide = held[...].reshape(rows, columns).astype(jnp.float32)
     squares = jnp.sum((wide * wide).reshape(rows // 8, 8, columns), axis=0)
     norm_mine[...] = sum(squares[:, at : at + 128] for at in range(0, columns, 128))
@@ -322,10 +400,12 @@
         core,
         part,
         2,
-        sib_two,
-        ready_two,
-        got_two,
-        (pair_sems.at[2], pair_sems.at[3], share_sems.at[2], share_sems.at[3]),
+        sib.at[1],
+        ready.at[1],
+        near_got.at[1],
+        far_ready.at[1],
+        far_got.at[1],
+        (pair_sems.at[1], near_sems.at[1], far_sems.at[1]),
     )
     sums = lax.fori_loop(1, sectors, norm_collect, norm_mine[...])
     count = float(sectors * rows * columns)
@@ -337,7 +417,7 @@
     chips = lax.axis_size("grp") // 2
     sectors = lax.axis_size("sector")
     columns = owned_rows.shape[-1]
-    shares = pltpu.VMEM((chips, SHARE, columns), jnp.bfloat16)
+    shares = (chips // NEAR, SHARE, columns)
     share = jax.ShapeDtypeStruct((SHARE, columns), jnp.bfloat16)
     return pl.pallas_call(
         functools.partial(step_kernel, chips, sectors),
@@ -345,19 +425,19 @@
         in_specs=[pl.BlockSpec(memory_space=pltpu.VMEM)] * 4,
         out_specs=[pl.BlockSpec(memory_space=pltpu.VMEM)] * 2,
         scratch_shapes=[
-            pltpu.VMEM((4, chips, SHARE, columns), jnp.bfloat16),
-            shares,
-            shares,
-            shares,
-            shares,
-            shares,
-            shares,
+            pltpu.VMEM((4, NEAR) + shares, jnp.bfloat16),
+            pltpu.VMEM((2, NEAR) + shares, jnp.bfloat16),
+            pltpu.VMEM((2, NEAR) + shares, jnp.bfloat16),
+            pltpu.VMEM((2, NEAR - 1) + shares, jnp.bfloat16),
+            pltpu.VMEM((2,) + shares, jnp.bfloat16),
+            pltpu.VMEM((2,) + shares, jnp.bfloat16),
             pltpu.VMEM((chips, 2, SHARE, columns), jnp.bfloat16),
             pltpu.VMEM((8, 128), jnp.float32),
             pltpu.VMEM((sectors, 8, 128), jnp.float32),
-            pltpu.SemaphoreType.DMA((4,)),
-            pltpu.SemaphoreType.DMA((4, chips)),
-            pltpu.SemaphoreType.DMA((4, chips)),
+            pltpu.SemaphoreType.DMA((2, 2, NEAR)),
+            pltpu.SemaphoreType.DMA((2, 2, NEAR)),
+            pltpu.SemaphoreType.DMA((2, 2, chips // NEAR)),
+            pltpu.SemaphoreType.DMA((4, 1, chips)),
             pltpu.SemaphoreType.DMA((2, sectors)),
         ],
         compiler_params=pltpu.CompilerParams(
@@ -511,10 +591,6 @@
         site_left.reshape(channels, WM, D1, D1) * mpo_pattern.astype(jnp.bfloat16)[:, :, None, None]
     )
     left_rows = left_site.transpose(2, 0, 3, 1).reshape(D1 * channels * D1, WM)
-    owned_rows, site_all, env_all = gather_all(start_vector, site_local, right_env)
-    mixing = build_mixing(
-        left_rows, site_all.reshape(WM, WM * PHYS), env_all.reshape(WM, RB * RB), channels
-    )
     owners = block_owner[:, :, 0]
     owner_hot = (owners[:, :, None] == jnp.arange(sectors, dtype=jnp.int32)[None, None, :]).astype(
         jnp.int32
@@ -537,9 +613,6 @@
     slots = channels * CAP
     packed = pack(
         pick.reshape(sectors * slots), env_blocks.reshape(channels * held_blocks, TR, TR)
-    )
-    got_codes = lax.all_to_all(
-        slot_codes.reshape(sectors, slots), "sector", split_axis=0, concat_axis=0, tiled=True
     )
     got_blocks = lax.all_to_all(
         packed.reshape(sectors, slots, TR, TR),
@@ -547,6 +620,12 @@
         split_axis=0,
         concat_axis=0,
         tiled=True,
+    )
+    owned_rows, site_all, env_all, got_codes = gather_all(
+        start_vector, site_local, right_env, slot_codes.reshape(sectors, 1, slots)
+    )
+    mixing = build_mixing(
+        left_rows, site_all.reshape(WM, WM * PHYS), env_all.reshape(WM, RB * RB), channels
     )
     dense = assemble(
         got_codes.reshape(sectors * slots), got_blocks.reshape(sectors * slots, TR, TR), channels

time: 145 us -> 129 us (0.89)
  the two profiles are of different devices: /device:TPU:52 before, /device:TPU:8 now
where the time goes in v3:
time: 129 us; the launch traced here: 128 us
  Pallas kernels  102 us (79%)
  local copies, waits for them, and re-layouts  10.7 us (8%)
  starting transfers between devices  10.1 us (8%)
  other arithmetic  4.79 us (4%)
    pallas_call x1, Pallas kernels, two_products(): pl.pallas_call(functools.partial(step_kernel, chips, sectors), out_shape=...  60.5 us
    pallas_call x1, Pallas kernels, gather_all(): pl.pallas_call(functools.partial(gather_kernel, chips, sectors), out_shap...  28.4 us
    all_to_all x1, starting transfers between devices, local(): lax.all_to_all(packed.reshape(sectors, slots, TR, TR), 'sector', split_ax...  10.1 us
    pallas_call x1, Pallas kernels, build_mixing(): pl.pallas_call(mixing_kernel, out_shape=jax.ShapeDtypeStruct((channels, c...  4.83 us
    pallas_call x1, Pallas kernels, assemble(): pl.pallas_call(assemble_kernel, out_shape=jax.ShapeDtypeStruct((channels,...  4.46 us
    pallas_call x1, Pallas kernels, pack(): pl.pallas_call(pack_kernel, out_shape=jax.ShapeDtypeStruct((pick.shape[0]...  3.97 us
  transfers between devices with their start and end apart: 1, of which 0 were waited for; matrix products, arithmetic and copies ran while one was open for 7% of the time, Pallas kernels for 26%

profile of v3, /device:TPU:8, one launch (start us, length us, event | category | flops | bytes accessed | tf_op | source)
XLA Modules:
  0.0 128.4 jit_solution(7499949121514959340)
XLA Ops:
  0.6 0.8 fusion
  1.4 0.9 select_reduce_fusion.2
  2.3 0.7 add_add_fusion
  3.0 0.7 fusion.2
  3.9 0.6 reshape.90.pick_ref
  4.5 4.0 %shard_map.114 = bf16[64,128,128]{2,1,0:T(8,128)(2,1)} custom-call(s32[64]{0:T(128)} %reshape.90.pick_ref, bf16[48,128,128]{2,1,0:T(8,128)(2,1)} %bitcast.20), custom_call_target="tpu_custom_call" | custom-call | tf_op jit(solution)/shard_map/pallas_call | solution.py:467
  8.5 10.1 %all-to-all-start = ((bf16[16,4,128,128]{3,2,1,0:T(8,128)(2,1)}), bf16[16,4,128,128]{3,2,1,0:T(8,128)(2,1)}, u32[]{:S(2)}, u32[]{:S(2)}) async-start(bf16[16,4,128,128]{3,2,1,0:T(8,128)(2,1)} %bitcast.19), calls=%async_computation | async-start | bytes 4194304 | tf_op jit(solution)/shard_map/all_to_all | solution.py:617
  18.6 0.3 reshape.84
  19.1 0.7 reshape.85.site_ref
  19.9 0.7 copy.28.code_ref
  20.6 28.4 %shard_map.113 = (bf16[16,2,16,512]{3,2,1,0:T(8,128)(2,1)}, bf16[16,2,2,1024]{3,2,1,0:T(2,128)(2,1)}, bf16[16,2,2,1024]{3,2,1,0:T(2,128)(2,1)}, s32[16,1,4]{2,1,0:T(1,128)}) custom-call(bf16[16,512]{1,0:T(8,128)(2,1)} %rows_ref.1, bf16[2,1024]{1,0:T(2,128)(2,1)} %reshape.85.site_ref, bf16[2,1024]{1,0:T(2,128)(2,1)} %env_ref.1, s32[16,1,4]{2,1,0:T(1,128)} %copy.28.code_ref), custom_call_target="tpu_custom_call" | custom-call | tf_op jit(solution)/shard_map/pallas_call | solution.py:221
  49.0 0.5 broadcast.30
  49.5 1.4 %reduce.3 = s32[16,4]{1,0:T(8,128)S(1)} reduce(s32[16,1,4]{2,1,0:T(1,128)} %get-tuple-element.6, s32[]{:T(128)} %broadcast.30), dimensions={1}, to_apply=%get-tuple-element.6.reduce_sub_computation.3 | reduce | bytes 516 | tf_op jit(solution)/shard_map/pallas_call | solution.py:221
  50.9 0.6 reshape.88.code_ref
  51.5 0.3 reshape.94
  52.0 0.7 copy.30
  52.7 1.6 %reshape.96.site_ref = bf16[64,1024]{1,0:T(8,128)(2,1)} reshape(bf16[16,2,2,1024]{3,2,1,0:T(2,128)(2,1)} %get-tuple-element.7) | data formatting | bytes 262144 | tf_op jit(solution)/shard_map/reshape | solution.py:628
  54.3 1.6 %reshape.97.env_ref = bf16[64,1024]{1,0:T(8,128)(2,1)} reshape(bf16[16,2,2,1024]{3,2,1,0:T(2,128)(2,1)} %get-tuple-element.8) | data formatting | bytes 262144 | tf_op jit(solution)/shard_map/reshape | solution.py:628
  56.2 4.8 %shard_map.116.mix_ref = bf16[2,512,512]{2,1,0:T(8,128)(2,1)} custom-call(bf16[32,64]{1,0:T(8,128)(2,1)} %bitcast.24, bf16[64,1024]{1,0:T(8,128)(2,1)} %reshape.96.site_ref, bf16[64,1024]{1,0:T(8,128)(2,1)} %reshape.97.env_ref), custom_call_target="tpu_custom_call" | custom-call | tf_op jit(solution)/shard_map/pallas_call | solution.py:563
  61.0 4.5 %shard_map.115.dense_ref = bf16[2,512,512]{2,1,0:T(8,128)(2,1)} custom-call(s32[64]{0:T(128)} %reshape.88.code_ref, bf16[64,128,128]{2,1,0:T(8,128)(2,1)} %bitcast.10.blocks_ref), custom_call_target="tpu_custom_call" | custom-call | tf_op jit(solution)/shard_map/pallas_call | solution.py:503
  65.5 1.2 copy-done.1
  66.7 60.5 %shard_map.117 = (bf16[16,512]{1,0:T(8,128)(2,1)S(1)}, bf16[16,512]{1,0:T(8,128)(2,1)S(1)}) custom-call(bf16[2,512,512]{2,1,0:T(8,128)(2,1)S(1)} %copy-done.1, bf16[2,512,512]{2,1,0:T(8,128)(2,1)S(1)} %copy-done, bf16[16,2,16,512]{3,2,1,0:T(8,128)(2,1)S(1)} %copy-done.2, f32[512,1]{1,0:T(8,128)S(1)} %copy.31.mask_ref), custom_call_target="tpu_custom_call" | custom-call | tf_op jit(solution)/shard_map/pallas_call | solution.py:422
  127.2 0.6 copy.34
  127.8 0.6 copy.35
  (25 shorter events, 1.0 us)
Async XLA Ops:
  8.5 10.1 %copy-start.3 = (bf16[2,1024]{1,0:T(2,128)(2,1)S(1)}, bf16[2,1024]{1,0:T(2,128)(2,1)}, u32[]{:S(2)}) copy-start(bf16[2,1024]{1,0:T(2,128)(2,1)} %param.18) | copy-start | bytes 12292
  8.5 43.0 %copy-start.4 = (bf16[2,1024]{1,0:T(2,128)(2,1)S(1)}, bf16[2,1024]{1,0:T(2,128)(2,1)}, u32[]{:S(2)}) copy-start(bf16[2,1024]{1,0:T(2,128)(2,1)} %param.16) | copy-start | bytes 12292
  8.5 43.3 %copy-start.6 = (s32[2,64]{1,0:T(2,128)S(1)}, s32[2,64]{1,0:T(2,128)}, u32[]{:S(2)}) copy-start(s32[2,64]{1,0:T(2,128)} %param.17) | copy-start | bytes 1540
  8.5 47.5 %copy-start.5 = (s32[4]{0:T(128)S(1)}, s32[4]{0:T(128)}, u32[]{:S(2)}) copy-start(s32[4]{0:T(128)} %param.11) | copy-start | bytes 52
  8.5 52.5 %all-to-all-start = ((bf16[16,4,128,128]{3,2,1,0:T(8,128)(2,1)}), bf16[16,4,128,128]{3,2,1,0:T(8,128)(2,1)}, u32[]{:S(2)}, u32[]{:S(2)}) async-start(bf16[16,4,128,128]{3,2,1,0:T(8,128)(2,1)} %bitcast.19), calls=%async_computation | async-start | bytes 4194304 | tf_op jit(solution)/shard_map/all_to_all | solution.py:617
  56.2 9.3 %copy-start.2 = (bf16[16,2,16,512]{3,2,1,0:T(8,128)(2,1)S(1)}, bf16[16,2,16,512]{3,2,1,0:T(8,128)(2,1)}, u32[]{:S(2)}) copy-start(bf16[16,2,16,512]{3,2,1,0:T(8,128)(2,1)} %get-tuple-element.9.start_ref) | copy-start | bytes 1572868
  61.0 4.5 %copy-start = (bf16[2,512,512]{2,1,0:T(8,128)(2,1)S(1)}, bf16[2,512,512]{2,1,0:T(8,128)(2,1)}, u32[]{:S(2)}) copy-start(bf16[2,512,512]{2,1,0:T(8,128)(2,1)} %shard_map.116.mix_ref) | copy-start | bytes 3145732
  65.5 1.2 copy-start.1

commit v4 on v3

--- a/solution.py
+++ b/solution.py
@@ -34,7 +34,7 @@
     )
 
 
-def greet(chips, chip, core, sectors=0):
+def greet(chips, chip, core, sectors):
     barrier = pltpu.get_barrier_semaphore()
 
     def greet_chip(step, carry):
@@ -48,22 +48,22 @@
     pl.semaphore_signal(
         barrier, inc=1, device_id={"grp": chip * 2 + 1 - core}, device_id_type=MESH
     )
-    if sectors:
-        owner = lax.axis_index("sector")
-
-        def greet_owner(step, carry):
-            pl.semaphore_signal(
-                barrier,
-                inc=1,
-                device_id={"sector": lax.rem(owner + step, sectors)},
-                device_id_type=MESH,
-            )
-            return carry
-
-        lax.fori_loop(1, sectors, greet_owner, 0)
-        pl.semaphore_wait(barrier, chips + sectors - 1)
-    else:
-        pl.semaphore_wait(barrier, chips)
+    owner = lax.axis_index("sector")
+
+    def greet_owner(step, carry):
+        pl.semaphore_signal(
+            barrier,
+            inc=1,
+            device_id={"sector": lax.rem(owner + step, sectors)},
+            device_id_type=MESH,
+        )
+        return carry
+
+    lax.fori_loop(1, sectors, greet_owner, 0)
+
+
+def await_greetings(chips, sectors):
+    pl.semaphore_wait(pltpu.get_barrier_semaphore(), chips + sectors - 1)
 
 
 NEAR = 4
@@ -180,10 +180,11 @@
     position = lax.axis_index("grp")
     owner = lax.axis_index("sector")
     chip, core = position // 2, lax.rem(position, 2)
+    greet(chips, chip, core, sectors)
     for source, target in ((rows_ref, rows_out), (site_ref, site_out), (env_ref, env_out)):
         target[chip, core] = source[...]
     code_out[owner] = code_ref[owner]
-    greet(chips, chip, core, sectors)
+    await_greetings(chips, sectors)
 
     def code_copy(step):
         other = lax.rem(owner + step, sectors)
@@ -325,11 +326,15 @@
     chips,
     sectors,
     dense_ref,
-    mix_ref,
+    left_ref,
+    site_ref,
+    env_ref,
     start_ref,
     mask_ref,
     first_out,
     second_out,
+    mix_ref,
+    wide_mix,
     part,
     sib,
     ready,
@@ -351,8 +356,10 @@
     rows = TPO * TR
     columns = start_ref.shape[-1]
     greet(chips, chip, core, sectors)
+    fill_mixing(left_ref, site_ref, env_ref, mix_ref, wide_mix)
     masked = start_ref[...].reshape(rows, columns) * mask_ref[...].astype(jnp.bfloat16)
     product(dense_ref, mix_ref, masked, part, 0)
+    await_greetings(chips, sectors)
     share_mask = mask_ref[pl.ds(pl.multiple_of(position * SHARE, SHARE), SHARE), :]
     total = reduce_share(
         chips,
@@ -413,7 +420,7 @@
     second_out[...] = (total * inverse_norm * share_mask).astype(jnp.bfloat16)
 
 
-def two_products(dense, mixing, owned_rows, owner_mask):
+def two_products(dense, left, site, env, owned_rows, owner_mask):
     chips = lax.axis_size("grp") // 2
     sectors = lax.axis_size("sector")
     columns = owned_rows.shape[-1]
@@ -422,9 +429,11 @@
     return pl.pallas_call(
         functools.partial(step_kernel, chips, sectors),
         out_shape=[share, share],
-        in_specs=[pl.BlockSpec(memory_space=pltpu.VMEM)] * 4,
+        in_specs=[pl.BlockSpec(memory_space=pltpu.VMEM)] * 6,
         out_specs=[pl.BlockSpec(memory_space=pltpu.VMEM)] * 2,
         scratch_shapes=[
+            pltpu.VMEM(dense.shape, jnp.bfloat16),
+            pltpu.VMEM((dense.shape[0] * D1, D1 * RB, columns), jnp.float32),
             pltpu.VMEM((4, NEAR) + shares, jnp.bfloat16),
             pltpu.VMEM((2, NEAR) + shares, jnp.bfloat16),
             pltpu.VMEM((2, NEAR) + shares, jnp.bfloat16),
@@ -443,7 +452,7 @@
         compiler_params=pltpu.CompilerParams(
             collective_id=1, has_side_effects=True, vmem_limit_bytes=40 * 1024 * 1024
         ),
-    )(dense, mixing, owned_rows, owner_mask)
+    )(dense, left, site, env, owned_rows, owner_mask)
 
 
 def pack_kernel(pick_ref, env_ref, out_ref):
@@ -512,7 +521,7 @@
     )(codes, blocks)
 
 
-def mixing_kernel(left_ref, site_ref, env_ref, out_ref, wide):
+def fill_mixing(left_ref, site_ref, env_ref, out_ref, wide):
     group = D1 * WM
     joined = jnp.concatenate(
         [
@@ -558,17 +567,6 @@
         )
 
 
-def build_mixing(left, site, env, channels):
-    columns = PHYS * RB
-    return pl.pallas_call(
-        mixing_kernel,
-        out_shape=jax.ShapeDtypeStruct((channels, columns, columns), jnp.bfloat16),
-        in_specs=[pl.BlockSpec(memory_space=pltpu.VMEM)] * 3,
-        out_specs=pl.BlockSpec(memory_space=pltpu.VMEM),
-        scratch_shapes=[pltpu.VMEM((channels * D1, D1 * RB, columns), jnp.float32)],
-    )(left, site, env)
-
-
 def local(
     start_vector,
     tile_live,
@@ -624,15 +622,21 @@
     owned_rows, site_all, env_all, got_codes = gather_all(
         start_vector, site_local, right_env, slot_codes.reshape(sectors, 1, slots)
     )
-    mixing = build_mixing(
-        left_rows, site_all.reshape(WM, WM * PHYS), env_all.reshape(WM, RB * RB), channels
-    )
     dense = assemble(
         got_codes.reshape(sectors * slots), got_blocks.reshape(sectors * slots, TR, TR), channels
     )
     tile_mask = (jnp.arange(TR, dtype=jnp.int32)[None, :] < tile_live[:, None]).reshape(TPO * TR)
     owner_mask = tile_mask.astype(jnp.float32)[:, None]
-    return tuple(two_products(dense, mixing, owned_rows, owner_mask))
+    return tuple(
+        two_products(
+            dense,
+            left_rows,
+            site_all.reshape(WM, WM * PHYS),
+            env_all.reshape(WM, RB * RB),
+            owned_rows,
+            owner_mask,
+        )
+    )
 
 
 def solution(mesh):

time: 129 us -> 123 us (0.953)
  Pallas kernels: 102 us -> 97.4 us
    pallas_call x1 -> x0, Pallas kernels: 4.83 us -> none  [build_mixing(): pl.pallas_call(mixing_kernel, out_shape=jax.ShapeDtypeStruct((channels, c...]
    unnamed x16, local copies, waits for them, and re-layouts: 2.46 us -> 3.8 us
  transfers between devices with their start and end apart: 1 -> 1, of which waited for: 0 -> 0; matrix products, arithmetic and copies ran while one was open for 7% -> 6% of each run, Pallas kernels for 26% -> 24%
where the time goes in v4:
time: 123 us
  Pallas kernels  97.4 us (79%)
  local copies, waits for them, and re-layouts  10.2 us (8%)
  starting transfers between devices  9.46 us (8%)
  other arithmetic  4.79 us (4%)
    pallas_call x1, Pallas kernels, two_products(): pl.pallas_call(functools.partial(step_kernel, chips, sectors), out_shape=...  60.1 us
    pallas_call x1, Pallas kernels, gather_all(): pl.pallas_call(functools.partial(gather_kernel, chips, sectors), out_shap...  28.9 us
    all_to_all x1, starting transfers between devices, local(): lax.all_to_all(packed.reshape(sectors, slots, TR, TR), 'sector', split_ax...  9.46 us
    pallas_call x1, Pallas kernels, assemble(): pl.pallas_call(assemble_kernel, out_shape=jax.ShapeDtypeStruct((channels,...  4.37 us
    pallas_call x1, Pallas kernels, pack(): pl.pallas_call(pack_kernel, out_shape=jax.ShapeDtypeStruct((pick.shape[0]...  4.03 us
    unnamed x16, local copies, waits for them, and re-layouts  3.8 us
  transfers between devices with their start and end apart: 1, of which 0 were waited for; matrix products, arithmetic and copies ran while one was open for 6% of the time, Pallas kernels for 24%

profile of v4, /device:TPU:8, one launch (start us, length us, event | category | flops | bytes accessed | tf_op | source)
XLA Modules:
  0.0 122.7 jit_solution(3038211119917961319)
XLA Ops:
  0.6 0.8 fusion
  1.4 0.9 select_reduce_fusion.2
  2.3 0.7 fusion.2
  3.0 0.7 add_add_fusion
  3.9 0.6 reshape.90.pick_ref
  4.5 4.0 %shard_map.114 = bf16[64,128,128]{2,1,0:T(8,128)(2,1)} custom-call(s32[64]{0:T(128)} %reshape.90.pick_ref, bf16[48,128,128]{2,1,0:T(8,128)(2,1)} %bitcast.22), custom_call_target="tpu_custom_call" | custom-call | tf_op jit(solution)/shard_map/pallas_call | solution.py:476
  8.6 9.5 %all-to-all-start = ((bf16[16,4,128,128]{3,2,1,0:T(8,128)(2,1)}), bf16[16,4,128,128]{3,2,1,0:T(8,128)(2,1)S(1)}, u32[]{:S(2)}, u32[]{:S(2)}) async-start(bf16[16,4,128,128]{3,2,1,0:T(8,128)(2,1)} %bitcast.21), calls=%async_computation | async-start | bytes 4194304 | tf_op jit(solution)/shard_map/all_to_all | solution.py:615
  18.2 0.7 copy.28.code_ref
  18.9 0.3 reshape.84
  19.3 0.7 reshape.85.site_ref
  20.0 28.9 %shard_map.113 = (bf16[16,2,16,512]{3,2,1,0:T(8,128)(2,1)}, bf16[16,2,2,1024]{3,2,1,0:T(2,128)(2,1)}, bf16[16,2,2,1024]{3,2,1,0:T(2,128)(2,1)}, s32[16,1,4]{2,1,0:T(1,128)}) custom-call(bf16[16,512]{1,0:T(8,128)(2,1)} %rows_ref.1, bf16[2,1024]{1,0:T(2,128)(2,1)} %reshape.85.site_ref, bf16[2,1024]{1,0:T(2,128)(2,1)} %env_ref.1, s32[16,1,4]{2,1,0:T(1,128)} %copy.28.code_ref), custom_call_target="tpu_custom_call" | custom-call | tf_op jit(solution)/shard_map/pallas_call | solution.py:222
  48.9 0.5 broadcast.30
  49.4 1.4 %reduce.3 = s32[16,4]{1,0:T(8,128)S(1)} reduce(s32[16,1,4]{2,1,0:T(1,128)} %get-tuple-element.6, s32[]{:T(128)} %broadcast.30), dimensions={1}, to_apply=%get-tuple-element.6.reduce_sub_computation.3 | reduce | bytes 516 | tf_op jit(solution)/shard_map/pallas_call | solution.py:222
  50.8 0.6 reshape.88.code_ref
  51.4 1.0 reshape.96.site_ref
  52.4 1.0 reshape.97.env_ref
  53.4 0.3 reshape.94
  53.7 0.2 multiply_bitcast_fusion
  54.3 1.3 %copy-done.2 = bf16[16,4,128,128]{3,2,1,0:T(8,128)(2,1)} copy-done((bf16[16,4,128,128]{3,2,1,0:T(8,128)(2,1)}, bf16[16,4,128,128]{3,2,1,0:T(8,128)(2,1)S(1)}, u32[]{:S(2)}) %copy-start.2) | copy-done | bytes 2097176
  55.7 4.4 %shard_map.115.dense_ref = bf16[2,512,512]{2,1,0:T(8,128)(2,1)} custom-call(s32[64]{0:T(128)} %reshape.88.code_ref, bf16[64,128,128]{2,1,0:T(8,128)(2,1)} %bitcast.20), custom_call_target="tpu_custom_call" | custom-call | tf_op jit(solution)/shard_map/pallas_call | solution.py:512
  60.1 1.2 copy-done
  61.3 60.1 %shard_map.116 = (bf16[16,512]{1,0:T(8,128)(2,1)S(1)}, bf16[16,512]{1,0:T(8,128)(2,1)S(1)}) custom-call(bf16[2,512,512]{2,1,0:T(8,128)(2,1)S(1)} %copy-done, bf16[32,64]{1,0:T(8,128)(2,1)S(1)} %bitcast.19, bf16[64,1024]{1,0:T(8,128)(2,1)S(1)} %reshape.96.site_ref, bf16[64,1024]{1,0:T(8,128)(2,1)S(1)} %reshape.97.env_ref, ...), custom_call_target="tpu_custom_call" | custom-call | tf_op jit(solution)/shard_map/pallas_call | solution.py:429
  121.4 0.6 copy.34
  122.0 0.6 copy.35
  (24 shorter events, 1.0 us)
Async XLA Ops:
  8.5 10.3 %copy-start.3 = (bf16[2,1024]{1,0:T(2,128)(2,1)S(1)}, bf16[2,1024]{1,0:T(2,128)(2,1)}, u32[]{:S(2)}) copy-start(bf16[2,1024]{1,0:T(2,128)(2,1)} %param.18) | copy-start | bytes 12292
  8.5 44.9 %copy-start.4 = (bf16[2,1024]{1,0:T(2,128)(2,1)S(1)}, bf16[2,1024]{1,0:T(2,128)(2,1)}, u32[]{:S(2)}) copy-start(bf16[2,1024]{1,0:T(2,128)(2,1)} %param.16) | copy-start | bytes 12292
  8.5 45.2 %copy-start.6 = (s32[2,64]{1,0:T(2,128)S(1)}, s32[2,64]{1,0:T(2,128)}, u32[]{:S(2)}) copy-start(s32[2,64]{1,0:T(2,128)} %param.17) | copy-start | bytes 1540
  8.5 45.5 %copy-start.5 = (s32[4]{0:T(128)S(1)}, s32[4]{0:T(128)}, u32[]{:S(2)}) copy-start(s32[4]{0:T(128)} %param.11) | copy-start | bytes 52
  8.6 45.8 %all-to-all-start = ((bf16[16,4,128,128]{3,2,1,0:T(8,128)(2,1)}), bf16[16,4,128,128]{3,2,1,0:T(8,128)(2,1)S(1)}, u32[]{:S(2)}, u32[]{:S(2)}) async-start(bf16[16,4,128,128]{3,2,1,0:T(8,128)(2,1)} %bitcast.21), calls=%async_computation | async-start | bytes 4194304 | tf_op jit(solution)/shard_map/all_to_all | solution.py:615
  52.4 7.7 %copy-start.1 = (bf16[16,2,16,512]{3,2,1,0:T(8,128)(2,1)S(1)}, bf16[16,2,16,512]{3,2,1,0:T(8,128)(2,1)}, u32[]{:S(2)}) copy-start(bf16[16,2,16,512]{3,2,1,0:T(8,128)(2,1)} %get-tuple-element.9.start_ref) | copy-start | bytes 1572868
  54.3 1.4 %copy-start.2 = (bf16[16,4,128,128]{3,2,1,0:T(8,128)(2,1)}, bf16[16,4,128,128]{3,2,1,0:T(8,128)(2,1)S(1)}, u32[]{:S(2)}) copy-start(bf16[16,4,128,128]{3,2,1,0:T(8,128)(2,1)S(1)} %all-to-all-done) | copy-start | bytes 6291460
  60.1 1.2 copy-start

commit v5 on v4

--- a/solution.py
+++ b/solution.py
@@ -253,7 +253,7 @@
     lax.fori_loop(0, TPO * TR // tile, one_tile, 0)
 
 
-def reduce_share(chips, chip, core, part, base, sib, ready, near_got, far_ready, far_got, sems):
+def reduce_share(chips, chip, core, part, base, sib, ready, near_got, far_ready, far_got, sems, meanwhile=None):
     pair_sems, near_sems, far_sems = sems
     ways = offsets(core)[::-1]
     far_count = chips // NEAR
@@ -303,6 +303,8 @@
     pair(NEAR - 1).wait_recv()
     kind = kind_of(NEAR - 1)
     total = part[base + core, kind].astype(jnp.float32) + sib[kind].astype(jnp.float32)
+    if meanwhile is not None:
+        meanwhile()
     for way in range(NEAR - 1):
         near(way).wait_recv()
         total += near_got[way].astype(jnp.float32)
@@ -378,10 +380,6 @@
     first_out[...] = first
     held[chip, core] = first
     spread((held,), chips, chip, core, [spread_sems.at[at] for at in range(4)])
-    wide = held[...].reshape(rows, columns).astype(jnp.float32)
-    squares = jnp.sum((wide * wide).reshape(rows // 8, 8, columns), axis=0)
-    norm_mine[...] = sum(squares[:, at : at + 128] for at in range(0, columns, 128))
-
     def norm_copy(step):
         return send_to(
             norm_mine,
@@ -399,7 +397,12 @@
         norm_copy(step).wait()
         return carry + norm_got[step]
 
-    lax.fori_loop(1, sectors, norm_start, 0)
+    def send_norm():
+        wide = held[...].reshape(rows, columns).astype(jnp.float32)
+        squares = jnp.sum((wide * wide).reshape(rows // 8, 8, columns), axis=0)
+        norm_mine[...] = sum(squares[:, at : at + 128] for at in range(0, columns, 128))
+        lax.fori_loop(1, sectors, norm_start, 0)
+
     product(dense_ref, mix_ref, held[...].reshape(rows, columns), part, 2)
     total = reduce_share(
         chips,
@@ -413,6 +416,7 @@
         far_ready.at[1],
         far_got.at[1],
         (pair_sems.at[1], near_sems.at[1], far_sems.at[1]),
+        send_norm,
     )
     sums = lax.fori_loop(1, sectors, norm_collect, norm_mine[...])
     count = float(sectors * rows * columns)
@@ -489,7 +493,7 @@
     channels = out_ref.shape[0]
 
     def one_slot(slot, carry):
-        code = code_ref[slot]
+        code = code_ref[slot // (channels * CAP), 0, lax.rem(slot, channels * CAP)]
         channel = lax.rem(slot // CAP, channels)
 
         @pl.when(code > 0)
@@ -623,7 +627,7 @@
         start_vector, site_local, right_env, slot_codes.reshape(sectors, 1, slots)
     )
     dense = assemble(
-        got_codes.reshape(sectors * slots), got_blocks.reshape(sectors * slots, TR, TR), channels
+        got_codes, got_blocks.reshape(sectors * slots, TR, TR), channels
     )
     tile_mask = (jnp.arange(TR, dtype=jnp.int32)[None, :] < tile_live[:, None]).reshape(TPO * TR)
     owner_mask = tile_mask.astype(jnp.float32)[:, None]

time: 123 us -> 120 us (0.976)
  other arithmetic: 4.79 us -> 3.43 us
    pallas_call x1 -> x0, other arithmetic: 1.37 us -> none  [gather_all(): pl.pallas_call(functools.partial(gather_kernel, chips, sectors), out_shap...]
  transfers between devices with their start and end apart: 1 -> 1, of which waited for: 0 -> 0; matrix products, arithmetic and copies ran while one was open for 6% -> 4% of each run, Pallas kernels for 24% -> 24%
where the time goes in v5:
time: 120 us
  Pallas kernels  97.2 us (81%)
  starting transfers between devices  9.46 us (8%)
  local copies, waits for them, and re-layouts  9.07 us (8%)
  other arithmetic  3.43 us (3%)
    pallas_call x1, Pallas kernels, two_products(): pl.pallas_call(functools.partial(step_kernel, chips, sectors), out_shape=...  59.9 us
    pallas_call x1, Pallas kernels, gather_all(): pl.pallas_call(functools.partial(gather_kernel, chips, sectors), out_shap...  28.9 us
    all_to_all x1, starting transfers between devices, local(): lax.all_to_all(packed.reshape(sectors, slots, TR, TR), 'sector', split_ax...  9.46 us
    pallas_call x1, Pallas kernels, assemble(): pl.pallas_call(assemble_kernel, out_shape=jax.ShapeDtypeStruct((channels,...  4.42 us
    pallas_call x1, Pallas kernels, pack(): pl.pallas_call(pack_kernel, out_shape=jax.ShapeDtypeStruct((pick.shape[0]...  4.02 us
    unnamed x16, local copies, waits for them, and re-layouts  3.79 us
  transfers between devices with their start and end apart: 1, of which 0 were waited for; matrix products, arithmetic and copies ran while one was open for 4% of the time, Pallas kernels for 24%

profile of v5, /device:TPU:8, one launch (start us, length us, event | category | flops | bytes accessed | tf_op | source)
XLA Modules:
  0.0 119.9 jit_solution(7347727544653251915)
XLA Ops:
  0.6 0.8 fusion
  1.4 0.9 select_reduce_fusion.2
  2.3 0.7 fusion.2
  3.0 0.7 add_add_fusion
  3.9 0.6 reshape.86.pick_ref
  4.5 4.0 %shard_map.114 = bf16[64,128,128]{2,1,0:T(8,128)(2,1)} custom-call(s32[64]{0:T(128)} %reshape.86.pick_ref, bf16[48,128,128]{2,1,0:T(8,128)(2,1)} %bitcast.22), custom_call_target="tpu_custom_call" | custom-call | tf_op jit(solution)/shard_map/pallas_call | solution.py:480
  8.5 9.5 %all-to-all-start = ((bf16[16,4,128,128]{3,2,1,0:T(8,128)(2,1)}), bf16[16,4,128,128]{3,2,1,0:T(8,128)(2,1)S(1)}, u32[]{:S(2)}, u32[]{:S(2)}) async-start(bf16[16,4,128,128]{3,2,1,0:T(8,128)(2,1)} %bitcast.21), calls=%async_computation | async-start | bytes 4194304 | tf_op jit(solution)/shard_map/all_to_all | solution.py:619
  18.2 0.7 copy.28.code_ref
  18.9 0.3 reshape.81
  19.2 0.1 copy.25
  19.3 0.7 reshape.82.site_ref
  20.0 28.9 %shard_map.113 = (bf16[16,2,16,512]{3,2,1,0:T(8,128)(2,1)}, bf16[16,2,2,1024]{3,2,1,0:T(2,128)(2,1)}, bf16[16,2,2,1024]{3,2,1,0:T(2,128)(2,1)}, s32[16,1,4]{2,1,0:T(1,128)}) custom-call(bf16[16,512]{1,0:T(8,128)(2,1)} %rows_ref.1, bf16[2,1024]{1,0:T(2,128)(2,1)} %reshape.82.site_ref, bf16[2,1024]{1,0:T(2,128)(2,1)} %env_ref.1, s32[16,1,4]{2,1,0:T(1,128)} %copy.28.code_ref), custom_call_target="tpu_custom_call" | custom-call | tf_op jit(solution)/shard_map/pallas_call | solution.py:222
  48.9 1.0 reshape.92.site_ref
  49.9 1.0 reshape.93.env_ref
  50.9 0.3 reshape.90
  51.2 0.2 multiply_bitcast_fusion
  51.4 0.1 copy.30
  51.7 0.2 copy.31.mask_ref
  51.8 1.3 %copy-done.2 = bf16[16,4,128,128]{3,2,1,0:T(8,128)(2,1)} copy-done((bf16[16,4,128,128]{3,2,1,0:T(8,128)(2,1)}, bf16[16,4,128,128]{3,2,1,0:T(8,128)(2,1)S(1)}, u32[]{:S(2)}) %copy-start.2) | copy-done | bytes 2097176
  53.2 4.4 %shard_map.115.dense_ref = bf16[2,512,512]{2,1,0:T(8,128)(2,1)} custom-call(s32[16,1,4]{2,1,0:T(1,128)} %get-tuple-element.6.code_ref, bf16[64,128,128]{2,1,0:T(8,128)(2,1)} %bitcast.20), custom_call_target="tpu_custom_call" | custom-call | tf_op jit(solution)/shard_map/pallas_call | solution.py:516
  57.6 1.2 %copy-done = bf16[2,512,512]{2,1,0:T(8,128)(2,1)S(1)} copy-done((bf16[2,512,512]{2,1,0:T(8,128)(2,1)S(1)}, bf16[2,512,512]{2,1,0:T(8,128)(2,1)}, u32[]{:S(2)}) %copy-start) | copy-done | bytes 1048600
  58.8 59.9 %shard_map.116 = (bf16[16,512]{1,0:T(8,128)(2,1)S(1)}, bf16[16,512]{1,0:T(8,128)(2,1)S(1)}) custom-call(bf16[2,512,512]{2,1,0:T(8,128)(2,1)S(1)} %copy-done, bf16[32,64]{1,0:T(8,128)(2,1)S(1)} %bitcast.19, bf16[64,1024]{1,0:T(8,128)(2,1)S(1)} %reshape.92.site_ref, bf16[64,1024]{1,0:T(8,128)(2,1)S(1)} %reshape.93.env_ref, ...), custom_call_target="tpu_custom_call" | custom-call | tf_op jit(solution)/shard_map/pallas_call | solution.py:433
  118.7 0.6 copy.34
  119.3 0.6 copy.35
  (21 shorter events, 0.5 us)
Async XLA Ops:
  8.5 10.3 %copy-start.3 = (bf16[2,1024]{1,0:T(2,128)(2,1)S(1)}, bf16[2,1024]{1,0:T(2,128)(2,1)}, u32[]{:S(2)}) copy-start(bf16[2,1024]{1,0:T(2,128)(2,1)} %param.18) | copy-start | bytes 12292
  8.5 42.4 %copy-start.4 = (bf16[2,1024]{1,0:T(2,128)(2,1)S(1)}, bf16[2,1024]{1,0:T(2,128)(2,1)}, u32[]{:S(2)}) copy-start(bf16[2,1024]{1,0:T(2,128)(2,1)} %param.16) | copy-start | bytes 12292
  8.5 42.7 %copy-start.6 = (s32[2,64]{1,0:T(2,128)S(1)}, s32[2,64]{1,0:T(2,128)}, u32[]{:S(2)}) copy-start(s32[2,64]{1,0:T(2,128)} %param.17) | copy-start | bytes 1540
  8.5 43.0 %copy-start.5 = (s32[4]{0:T(128)S(1)}, s32[4]{0:T(128)}, u32[]{:S(2)}) copy-start(s32[4]{0:T(128)} %param.11) | copy-start | bytes 52
  8.5 43.3 %all-to-all-start = ((bf16[16,4,128,128]{3,2,1,0:T(8,128)(2,1)}), bf16[16,4,128,128]{3,2,1,0:T(8,128)(2,1)S(1)}, u32[]{:S(2)}, u32[]{:S(2)}) async-start(bf16[16,4,128,128]{3,2,1,0:T(8,128)(2,1)} %bitcast.21), calls=%async_computation | async-start | bytes 4194304 | tf_op jit(solution)/shard_map/all_to_all | solution.py:619
  49.9 7.7 %copy-start.1 = (bf16[16,2,16,512]{3,2,1,0:T(8,128)(2,1)S(1)}, bf16[16,2,16,512]{3,2,1,0:T(8,128)(2,1)}, u32[]{:S(2)}) copy-start(bf16[16,2,16,512]{3,2,1,0:T(8,128)(2,1)} %get-tuple-element.9.start_ref) | copy-start | bytes 1572868
  51.8 1.3 %copy-start.2 = (bf16[16,4,128,128]{3,2,1,0:T(8,128)(2,1)}, bf16[16,4,128,128]{3,2,1,0:T(8,128)(2,1)S(1)}, u32[]{:S(2)}) copy-start(bf16[16,4,128,128]{3,2,1,0:T(8,128)(2,1)S(1)} %all-to-all-done) | copy-start | bytes 6291460
  57.6 1.2 %copy-start = (bf16[2,512,512]{2,1,0:T(8,128)(2,1)S(1)}, bf16[2,512,512]{2,1,0:T(8,128)(2,1)}, u32[]{:S(2)}) copy-start(bf16[2,512,512]{2,1,0:T(8,128)(2,1)} %shard_map.115.dense_ref) | copy-start | bytes 3145732
